TPU v7x, 1024 devices: a whole 4x8x16 slice. The times are simulated.
1024 devices in a mesh: gx: 32 (over x_hi, z), gy: 32 (over x_lo, y, core).
Axes of the slice: x: 4 (x_hi: 2, x_lo: 2; x = x_hi * 2 + x_lo), y: 8, z: 16, core: 2. Of those that a mesh axis runs over, the one named last changes fastest.
Arguments:
- velocity: float32 [3, 8, 1024, 4096], P(None, None, 'gx', 'gy'), may hold values from -6 to 6
- stress: float32 [6, 8, 1024, 4096], P(None, None, 'gx', 'gy'), may hold values from -6 to 6
- zones: int32 [8, 1024, 4096], P(None, 'gx', 'gy'), may hold values from 0 to 15
- zone_table: float32 [3, 16], replicated, may hold values from 0.5 to 2
- regional: float32 [32, 2, 3, 32, 8192], P('gx', None, None, None, 'gy'), may hold values from -6 to 6
- owner: int32 [32], replicated, may hold values from 0 to 31
- footprint_building: int32 [32, 32, 64], P('gx', 'gy'), may hold values from 0 to 1023
- footprint_block: int32 [32, 32, 64], P('gx', 'gy'), may hold values from 0 to 63
Outputs:
- velocity_out: float32 [3, 8, 1024, 4096], P(None, None, 'gx', 'gy')
- stress_out: float32 [6, 8, 1024, 4096], P(None, None, 'gx', 'gy')
- base_shear: float32 [2, 1024], replicated
All inputs are finite; a program needn't handle non-finite values.
Results may differ from a plain program's by a relative error of at most 0.000084.
Values sent between devices are 32-bit elements; how exact they have to be, the bound alone decides.
A program may use at most 32 MiB of HBM per device.

v0:
```python
import jax
import jax.numpy as jnp
from jax import lax
from jax.sharding import PartitionSpec as P

CX = 32
CY = 128
NZ = 8
STEPS = 2
COARSE = 4
BLOCK = 8
ZONES = 16
BUILDINGS = 1024


def with_halo(value, sides, width):
    for axis, dim in sides:
        devices, length = (lax.axis_size(axis), value.shape[dim])
        up = [(i, (i + 1) % devices) for i in range(devices)]
        down = [(j, i) for i, j in up]
        last = lax.slice_in_dim(value, length - width, length, axis=dim)
        leading = lax.slice_in_dim(value, 0, width, axis=dim)
        before = lax.ppermute(last, axis, up)
        after = lax.ppermute(leading, axis, down)
        value = jnp.concatenate([before, value, after], axis=dim)
    return value


def broadcast(value, axis, source):
    kept = jnp.where(lax.axis_index(axis) == source, value, 0).astype(value.dtype)
    return lax.psum(kept, axis)


def diff_z(field):
    padded = jnp.pad(field, ((1, 1), (0, 0), (0, 0)))
    return (padded[2:] - padded[:-2]) * 0.5


def lookup(zones, column):
    total = jnp.zeros(zones.shape, jnp.float32)
    for zone in range(ZONES):
        total = total + jnp.where(zones == zone, column[zone], 0.0)
    return total


def stress_slopes(stress):
    padded = with_halo(stress, (("gx", 2), ("gy", 3)), 1)
    along_x = (padded[0:3, :, 2:, 1:-1] - padded[0:3, :, :-2, 1:-1]) * 0.5
    along_y = (padded[2:5, :, 1:-1, 2:] - padded[2:5, :, 1:-1, :-2]) * 0.5
    return (along_x, along_y)


def body(velocity, stress, zones, zone_table, regional, owner, footprint_building, footprint_block):
    lam = lookup(zones, zone_table[0])
    shear_mod = lookup(zones, zone_table[1])
    buoy = lookup(zones, zone_table[2])
    root = owner[lax.axis_index("gy")]
    columns_all = broadcast(regional[0], "gx", root)
    mine = lax.dynamic_index_in_dim(columns_all, lax.axis_index("gx"), 2, keepdims=False)
    coarse = mine.reshape(STEPS, 3, CX // COARSE, CY // COARSE)
    drm = jnp.repeat(jnp.repeat(coarse, COARSE, axis=2), COARSE, axis=3)
    for step in range(STEPS):
        along_x, along_y = stress_slopes(stress)
        force_x = along_x[0] + along_y[0] + diff_z(stress[1])
        force_y = along_x[2] + along_y[1] + diff_z(stress[4])
        force_z = along_x[1] + along_y[2] + diff_z(stress[5])
        force = jnp.stack([force_x, force_y, force_z])
        force = force.at[:, NZ - 1].add(shear_mod[NZ - 1][None] * drm[step])
        velocity = velocity + 0.2 * buoy[None] * force
        padded = with_halo(velocity, (("gx", 2), ("gy", 3)), 1)
        vel_x = (padded[:, :, 2:, 1:-1] - padded[:, :, :-2, 1:-1]) * 0.5
        vel_y = (padded[:, :, 1:-1, 2:] - padded[:, :, 1:-1, :-2]) * 0.5
        dvx_dx = vel_x[0]
        dvy_dy = vel_y[1]
        dvz_dz = diff_z(velocity[2])
        theta = dvx_dx + dvy_dy + dvz_dz
        new_xx = stress[0] + 0.2 * (lam * theta + 2.0 * shear_mod * dvx_dx)
        new_xz = stress[1] + 0.2 * shear_mod * (diff_z(velocity[0]) + vel_x[2])
        new_xy = stress[2] + 0.2 * shear_mod * (vel_y[0] + vel_x[1])
        new_yy = stress[3] + 0.2 * (lam * theta + 2.0 * shear_mod * dvy_dy)
        new_yz = stress[4] + 0.2 * shear_mod * (diff_z(velocity[1]) + vel_y[2])
        new_zz = stress[5] + 0.2 * (lam * theta + 2.0 * shear_mod * dvz_dz)
        stress = jnp.stack([new_xx, new_xz, new_xy, new_yy, new_yz, new_zz])
    plane = jnp.stack([stress[1, 1], stress[4, 1]])
    plane = plane.reshape(2, CX // BLOCK, BLOCK, CY // BLOCK, BLOCK)
    means = (jnp.sum(plane, axis=(2, 4)) * (1.0 / (BLOCK * BLOCK))).reshape(2, -1)
    block_ids = footprint_block[0, 0]
    building_ids = footprint_building[0, 0]
    block_table = (
        block_ids[:, None] == jnp.arange(means.shape[1], dtype=jnp.int32)[None, :]
    ).astype(jnp.float32)
    values = jnp.dot(means, block_table.T, precision=lax.Precision.HIGHEST)
    building_table = (
        building_ids[:, None] == jnp.arange(BUILDINGS, dtype=jnp.int32)[None, :]
    ).astype(jnp.float32)
    partial_shear = jnp.dot(values, building_table, precision=lax.Precision.HIGHEST)
    shear = lax.psum(partial_shear, ("gx", "gy"))
    return (velocity, stress, shear)


def solution(mesh):
    return jax.shard_map(
        body,
        mesh=mesh,
        in_specs=(
            P(None, None, "gx", "gy"),
            P(None, None, "gx", "gy"),
            P(None, "gx", "gy"),
            P(),
            P("gx", None, None, None, "gy"),
            P(),
            P("gx", "gy", None),
            P("gx", "gy", None),
        ),
        out_specs=(P(None, None, "gx", "gy"), P(None, None, "gx", "gy"), P()),
        check_vma=False,
    )
```

profile of v0, /device:TPU:1, one launch (start us, length us, event | category | flops | bytes accessed | tf_op | source)
XLA Modules:
  0.0 556.1 jit_solution(9341403836314427009)
XLA Ops:
  7.2 1.1 fusion.93
  8.3 4.8 collective-permute-start.1
  13.1 18.3 %collective-permute-start = (f32[6,8,1,128]{3,1,2,0:T(8,128)S(1)}, f32[6,8,1,128]{3,1,2,0:T(8,128)}, u32[]{:S(2)}, u32[]{:S(2)}) collective-permute-start(f32[6,8,1,128]{3,1,2,0:T(8,128)S(1)} %bitcast.288), channel_id=1, source_target_pairs={{32,0},{64,32},{96,64},{128,96},{160,128},{192,160},{224,192},{256... | collective-permute-start | bytes 73736 | tf_op jit(solution)/shard_map/ppermute | solution.py:24
  33.3 1.6 select_bitcast_fusion
  35.7 0.7 fusion.99
  37.1 0.7 fusion.98
  37.8 10.3 %add_multiply_fusion.2 = (f32[8,32,128]{2,1,0:T(8,128)S(1)}, pred[8,32,128]{2,1,0:T(8,128)(4,1)S(1)}, pred[8,32,128]{2,1,0:T(8,128)(4,1)S(1)}, pred[8,32,128]{2,...) fusion(f32[]{:T(128)} %bitcast.15, f32[]{:T(128)} %bitcast.14, ...), kind=kLoop, calls=%fused_computation.190 | loop fusion | flops 1572864 | bytes 786496 | tf_op jit(solution)/shard_map/mul | solution.py:69
  48.7 10.5 %select_add_fusion.1 = f32[8,32,128]{2,1,0:T(8,128)S(1)} fusion(pred[8,32,128]{2,1,0:T(8,128)(4,1)S(1)} %get-tuple-element.78, pred[8,32,128]{2,1,0:T(8,128)(4,1)S(1)} %get-tuple-element.77, pred[8,32,128]{2,1,0:T(8,128)(4,1)S(1)} %get-tuple-element.76, pred[8,32,128]{2,1,0:T(8,128)(4,1)S(1)} %get-tuple-element.75, ...), kind=kLoop, calls=%fused_computation.186 | loop fusion | flops 1015808 | bytes 655424 | tf_op jit(solution)/shard_map/add | solution.py:42
  59.4 0.7 slice_bitcast_fusion.16
  60.1 0.9 pad_maximum_fusion
  61.8 3.1 collective-permute-start.3
  65.3 1.9 collective-permute-start.2
  67.7 3.1 collective-permute-done.2
  71.4 1.3 fusion.15
  72.8 227.2 %all-reduce.14.cloned.1.call-done = f32[2,3,32,256]{3,2,1,0:T(8,128)} async-done(((f32[2,3,32,256]{3,2,1,0:T(8,128)}), f32[2,3,32,256]{3,2,1,0:T(8,128)}) %all-reduce.14.cloned.1.call-update) | async-done | bytes 196624 | tf_op jit(solution)/shard_map/psum | solution.py:31
  300.0 1.4 dynamic-slice_reduce_fusion
  301.7 0.7 copy-done.13
  302.6 6.0 %collective-permute-start.4 = (f32[3,8,1,128]{3,1,2,0:T(8,128)S(1)}, f32[3,8,1,128]{3,1,2,0:T(8,128)S(1)}, u32[]{:S(2)}, u32[]{:S(2)}) collective-permute-start(f32[3,8,1,128]{3,1,2,0:T(8,128)S(1)} %bitcast.294), channel_id=1, source_target_pairs={{32,0},{64,32},{96,64},{128,96},{160,128},{192,160},{224,192},{256... | collective-permute-start | bytes 36872 | tf_op jit(solution)/shard_map/ppermute | solution.py:24
  308.6 1.9 collective-permute-start.5
  310.6 6.1 %collective-permute-done.5 = f32[3,8,1,128]{3,1,2,0:T(8,128)S(1)} collective-permute-done((f32[3,8,1,128]{3,1,2,0:T(8,128)S(1)}, f32[3,8,1,128]{3,1,2,0:T(8,128)S(1)}, u32[]{:S(2)}, u32[]{:S(2)}) %collective-permute-start.5) | collective-permute-done | bytes 12320 | tf_op jit(solution)/shard_map/ppermute | solution.py:23
  316.9 23.1 %collective-permute-start.7 = (f32[3,8,34,1]{3,2,1,0:T(8,128)S(1)}, f32[3,8,34,1]{3,2,1,0:T(8,128)S(1)}, u32[]{:S(2)}, u32[]{:S(2)}) collective-permute-start(f32[3,8,34,1]{3,2,1,0:T(8,128)S(1)} %get-tuple-element.103), channel_id=1, source_target_pairs={{0,1},{1,2},{2,3},{3,4},{4,5},{5,6},{6,7},{7,8},{8,9},{9,10},{10,1... | collective-permute-start | bytes 9800 | tf_op jit(solution)/shard_map/ppermute | solution.py:23
  340.0 1.9 collective-permute-start.6
  342.0 3.8 collective-permute-done.7
  345.8 4.4 collective-permute-done.6
  351.7 10.6 %bitcast_dynamic-update-slice_fusion.8 = (f32[6,8,32,128]{3,2,1,0:T(8,128)S(1)}, f32[8,32,128]{2,1,0:T(8,128)S(1)}, f32[8,32,128]{2,1,0:T(8,128)}) fusion(f32[3,8,32,128]{3,2,1,0:T(8,128)S(1)} %get-tuple-element.107, f32[8,32,128]{2,1,0:T(8,128)S(1)} %select_add_fusion.1, f32[6,8,32,128]{3,2,1,0:T(8,128)S(1)} %copy-done, ...), kind=kLoop, calls=%fused_computation.179 | loop fusion | flops 1343487 | bytes 1572928
  362.4 0.7 bitcast_dynamic-update-slice_fusion.7
  363.2 0.7 bitcast_dynamic-update-slice_fusion.4
  363.9 0.7 bitcast_dynamic-update-slice_fusion.3
  364.6 1.9 collective-permute-start.9
  366.6 7.0 %collective-permute-start.8 = (f32[6,8,1,128]{3,1,2,0:T(8,128)S(1)}, f32[6,8,1,128]{3,1,2,0:T(8,128)S(1)}, u32[]{:S(2)}, u32[]{:S(2)}) collective-permute-start(f32[6,8,1,128]{3,1,2,0:T(8,128)S(1)} %bitcast.290), channel_id=1, source_target_pairs={{32,0},{64,32},{96,64},{128,96},{160,128},{192,160},{224,192},{256... | collective-permute-start | bytes 73736 | tf_op jit(solution)/shard_map/ppermute | solution.py:24
  373.6 0.9 collective-permute-done.8
  375.1 0.9 pad_maximum_fusion.1
  376.3 1.0 copy.459
  377.3 2.9 collective-permute-start.11
  380.6 2.9 collective-permute-start.10
  383.8 0.7 copy.462
  385.0 1.1 collective-permute-done.10
  386.1 1.2 copy.458
  387.3 1.9 fusion.7
  389.4 0.8 copy-done.47
  390.3 7.5 %collective-permute-start.12 = (f32[3,8,1,128]{3,1,2,0:T(8,128)S(1)}, f32[3,8,1,128]{3,1,2,0:T(8,128)S(1)}, u32[]{:S(2)}, u32[]{:S(2)}) collective-permute-start(f32[3,8,1,128]{3,1,2,0:T(8,128)S(1)} %bitcast.295), channel_id=1, source_target_pairs={{32,0},{64,32},{96,64},{128,96},{160,128},{192,160},{224,192},{256... | collective-permute-start | bytes 36872 | tf_op jit(solution)/shard_map/ppermute | solution.py:24
  397.8 1.9 collective-permute-start.13
  399.8 6.1 %collective-permute-done.13 = f32[3,8,1,128]{3,1,2,0:T(8,128)S(1)} collective-permute-done((f32[3,8,1,128]{3,1,2,0:T(8,128)S(1)}, f32[3,8,1,128]{3,1,2,0:T(8,128)S(1)}, u32[]{:S(2)}, u32[]{:S(2)}) %collective-permute-start.13) | collective-permute-done | bytes 12320 | tf_op jit(solution)/shard_map/ppermute | solution.py:23
  406.2 3.1 collective-permute-start.15
  409.2 5.0 collective-permute-start.14
  415.0 4.7 collective-permute-done.14
  420.3 0.9 copy-done.4
  423.9 125.3 %psum.15 = f32[2,1024]{1,0:T(2,128)} all-reduce(f32[2,1024]{1,0:T(2,128)S(1)} %fusion.16), channel_id=1, replica_groups=mesh['gx'=32,'gy'=32] {'gx','gy'}, use_global_device_ids=true, to_apply=%region_2.3 | all-reduce | flops 2048 | bytes 16384 | tf_op jit(solution)/shard_map/psum | solution.py:97
  (173 shorter events, 14.2 us)
Async XLA Ops:
  7.2 292.9 %all-reduce.14.cloned.1.call-start = ((), (), s32[]{:S(2)}) async-start(), calls=%async_computation | async-start | bytes 393216 | tf_op jit(solution)/shard_map/psum | solution.py:31
  8.3 51.9 %collective-permute-start.1 = (f32[6,8,1,128]{3,1,2,0:T(8,128)S(1)}, f32[6,8,1,128]{3,1,2,0:T(8,128)}, u32[]{:S(2)}, u32[]{:S(2)}) collective-permute-start(f32[6,8,1,128]{3,1,2,0:T(8,128)S(1)} %bitcast.289), channel_id=1, source_target_pairs={{0,32},{32,64},{64,96},{96,128},{128,160},{160,192},{192,224},{224... | collective-permute-start | bytes 73736 | tf_op jit(solution)/shard_map/ppermute | solution.py:23
  13.1 47.0 %collective-permute-start = (f32[6,8,1,128]{3,1,2,0:T(8,128)S(1)}, f32[6,8,1,128]{3,1,2,0:T(8,128)}, u32[]{:S(2)}, u32[]{:S(2)}) collective-permute-start(f32[6,8,1,128]{3,1,2,0:T(8,128)S(1)} %bitcast.288), channel_id=1, source_target_pairs={{32,0},{64,32},{96,64},{128,96},{160,128},{192,160},{224,192},{256... | collective-permute-start | bytes 73736 | tf_op jit(solution)/shard_map/ppermute | solution.py:24
  35.0 2.8 copy-start.48
  37.8 21.6 %copy-start = (f32[6,8,32,128]{3,2,1,0:T(8,128)S(1)}, f32[6,8,32,128]{3,2,1,0:T(8,128)}, u32[]{:S(2)}) copy-start(f32[6,8,32,128]{3,2,1,0:T(8,128)} %param.13) | copy-start | bytes 2359300
  48.1 11.1 %copy-start.19 = (pred[8,32,128]{2,1,0:T(8,128)(4,1)}, pred[8,32,128]{2,1,0:T(8,128)(4,1)S(1)}, u32[]{:S(2)}) copy-start(pred[8,32,128]{2,1,0:T(8,128)(4,1)S(1)} %get-tuple-element.65) | copy-start | bytes 98308
  48.1 11.1 %copy-start.21 = (pred[8,32,128]{2,1,0:T(8,128)(4,1)}, pred[8,32,128]{2,1,0:T(8,128)(4,1)S(1)}, u32[]{:S(2)}) copy-start(pred[8,32,128]{2,1,0:T(8,128)(4,1)S(1)} %get-tuple-element.66) | copy-start | bytes 98308
  48.2 11.1 %copy-start.23 = (pred[8,32,128]{2,1,0:T(8,128)(4,1)}, pred[8,32,128]{2,1,0:T(8,128)(4,1)S(1)}, u32[]{:S(2)}) copy-start(pred[8,32,128]{2,1,0:T(8,128)(4,1)S(1)} %get-tuple-element.67) | copy-start | bytes 98308
  48.2 11.1 %copy-start.25 = (pred[8,32,128]{2,1,0:T(8,128)(4,1)}, pred[8,32,128]{2,1,0:T(8,128)(4,1)S(1)}, u32[]{:S(2)}) copy-start(pred[8,32,128]{2,1,0:T(8,128)(4,1)S(1)} %get-tuple-element.68) | copy-start | bytes 98308
  48.2 11.1 %copy-start.27 = (pred[8,32,128]{2,1,0:T(8,128)(4,1)}, pred[8,32,128]{2,1,0:T(8,128)(4,1)S(1)}, u32[]{:S(2)}) copy-start(pred[8,32,128]{2,1,0:T(8,128)(4,1)S(1)} %get-tuple-element.69) | copy-start | bytes 98308
  48.2 11.1 %copy-start.29 = (pred[8,32,128]{2,1,0:T(8,128)(4,1)}, pred[8,32,128]{2,1,0:T(8,128)(4,1)S(1)}, u32[]{:S(2)}) copy-start(pred[8,32,128]{2,1,0:T(8,128)(4,1)S(1)} %get-tuple-element.70) | copy-start | bytes 98308
  48.2 11.1 %copy-start.31 = (pred[8,32,128]{2,1,0:T(8,128)(4,1)}, pred[8,32,128]{2,1,0:T(8,128)(4,1)S(1)}, u32[]{:S(2)}) copy-start(pred[8,32,128]{2,1,0:T(8,128)(4,1)S(1)} %get-tuple-element.71) | copy-start | bytes 98308
  48.2 11.1 %copy-start.33 = (pred[8,32,128]{2,1,0:T(8,128)(4,1)}, pred[8,32,128]{2,1,0:T(8,128)(4,1)S(1)}, u32[]{:S(2)}) copy-start(pred[8,32,128]{2,1,0:T(8,128)(4,1)S(1)} %get-tuple-element.72) | copy-start | bytes 98308
  48.2 11.1 %copy-start.35 = (pred[8,32,128]{2,1,0:T(8,128)(4,1)}, pred[8,32,128]{2,1,0:T(8,128)(4,1)S(1)}, u32[]{:S(2)}) copy-start(pred[8,32,128]{2,1,0:T(8,128)(4,1)S(1)} %get-tuple-element.73) | copy-start | bytes 98308
  48.2 11.1 %copy-start.37 = (pred[8,32,128]{2,1,0:T(8,128)(4,1)}, pred[8,32,128]{2,1,0:T(8,128)(4,1)S(1)}, u32[]{:S(2)}) copy-start(pred[8,32,128]{2,1,0:T(8,128)(4,1)S(1)} %get-tuple-element.74) | copy-start | bytes 98308
  48.2 11.1 %copy-start.39 = (pred[8,32,128]{2,1,0:T(8,128)(4,1)}, pred[8,32,128]{2,1,0:T(8,128)(4,1)S(1)}, u32[]{:S(2)}) copy-start(pred[8,32,128]{2,1,0:T(8,128)(4,1)S(1)} %get-tuple-element.75) | copy-start | bytes 98308
  48.2 11.1 %copy-start.41 = (pred[8,32,128]{2,1,0:T(8,128)(4,1)}, pred[8,32,128]{2,1,0:T(8,128)(4,1)S(1)}, u32[]{:S(2)}) copy-start(pred[8,32,128]{2,1,0:T(8,128)(4,1)S(1)} %get-tuple-element.76) | copy-start | bytes 98308
  48.3 11.1 %copy-start.43 = (pred[8,32,128]{2,1,0:T(8,128)(4,1)}, pred[8,32,128]{2,1,0:T(8,128)(4,1)S(1)}, u32[]{:S(2)}) copy-start(pred[8,32,128]{2,1,0:T(8,128)(4,1)S(1)} %get-tuple-element.77) | copy-start | bytes 98308
  48.3 11.1 %copy-start.45 = (pred[8,32,128]{2,1,0:T(8,128)(4,1)}, pred[8,32,128]{2,1,0:T(8,128)(4,1)S(1)}, u32[]{:S(2)}) copy-start(pred[8,32,128]{2,1,0:T(8,128)(4,1)S(1)} %get-tuple-element.78) | copy-start | bytes 98308
  61.8 5.5 collective-permute-start.3
  65.3 5.5 collective-permute-start.2
  71.3 1.3 copy-start.11
  71.3 1.3 copy-start.12
  301.5 1.0 copy-start.13
  302.6 8.0 %collective-permute-start.4 = (f32[3,8,1,128]{3,1,2,0:T(8,128)S(1)}, f32[3,8,1,128]{3,1,2,0:T(8,128)S(1)}, u32[]{:S(2)}, u32[]{:S(2)}) collective-permute-start(f32[3,8,1,128]{3,1,2,0:T(8,128)S(1)} %bitcast.294), channel_id=1, source_target_pairs={{32,0},{64,32},{96,64},{128,96},{160,128},{192,160},{224,192},{256... | collective-permute-start | bytes 36872 | tf_op jit(solution)/shard_map/ppermute | solution.py:24
  308.6 8.1 %collective-permute-start.5 = (f32[3,8,1,128]{3,1,2,0:T(8,128)S(1)}, f32[3,8,1,128]{3,1,2,0:T(8,128)S(1)}, u32[]{:S(2)}, u32[]{:S(2)}) collective-permute-start(f32[3,8,1,128]{3,1,2,0:T(8,128)S(1)} %bitcast.292), channel_id=1, source_target_pairs={{0,32},{32,64},{64,96},{96,128},{128,160},{160,192},{192,224},{224... | collective-permute-start | bytes 36872 | tf_op jit(solution)/shard_map/ppermute | solution.py:23
  316.9 28.9 %collective-permute-start.7 = (f32[3,8,34,1]{3,2,1,0:T(8,128)S(1)}, f32[3,8,34,1]{3,2,1,0:T(8,128)S(1)}, u32[]{:S(2)}, u32[]{:S(2)}) collective-permute-start(f32[3,8,34,1]{3,2,1,0:T(8,128)S(1)} %get-tuple-element.103), channel_id=1, source_target_pairs={{0,1},{1,2},{2,3},{3,4},{4,5},{5,6},{6,7},{7,8},{8,9},{9,10},{10,1... | collective-permute-start | bytes 9800 | tf_op jit(solution)/shard_map/ppermute | solution.py:23
  340.0 10.1 %collective-permute-start.6 = (f32[3,8,34,1]{3,2,1,0:T(8,128)S(1)}, f32[3,8,34,1]{3,2,1,0:T(8,128)S(1)}, u32[]{:S(2)}, u32[]{:S(2)}) collective-permute-start(f32[3,8,34,1]{3,2,1,0:T(8,128)S(1)} %get-tuple-element.102), channel_id=1, source_target_pairs={{1,0},{2,1},{3,2},{4,3},{5,4},{6,5},{7,6},{8,7},{9,8},{10,9},{11,1... | collective-permute-start | bytes 9800 | tf_op jit(solution)/shard_map/ppermute | solution.py:24
  350.8 12.3 %copy-start.5 = (f32[3,8,32,128]{3,2,1,0:T(8,128)}, f32[3,8,32,128]{3,2,1,0:T(8,128)S(1)}, u32[]{:S(2)}) copy-start(f32[3,8,32,128]{3,2,1,0:T(8,128)S(1)} %get-tuple-element.107) | copy-start | bytes 1179652
  350.8 12.4 %copy-start.3 = (f32[3,8,32,128]{3,2,1,0:T(8,128)}, f32[3,8,32,128]{3,2,1,0:T(8,128)S(1)}, u32[]{:S(2)}) copy-start(f32[3,8,32,128]{3,2,1,0:T(8,128)S(1)} %get-tuple-element.106) | copy-start | bytes 1179652
  364.6 9.9 %copy-start.2 = (f32[6,8,32,128]{3,2,1,0:T(8,128)}, f32[6,8,32,128]{3,2,1,0:T(8,128)S(1)}, u32[]{:S(2)}) copy-start(f32[6,8,32,128]{3,2,1,0:T(8,128)S(1)} %get-tuple-element.53) | copy-start | bytes 2359300
  364.6 8.9 %collective-permute-start.9 = (f32[6,8,1,128]{3,1,2,0:T(8,128)S(1)}, f32[6,8,1,128]{3,1,2,0:T(8,128)}, u32[]{:S(2)}, u32[]{:S(2)}) collective-permute-start(f32[6,8,1,128]{3,1,2,0:T(8,128)S(1)} %bitcast.291), channel_id=1, source_target_pairs={{0,32},{32,64},{64,96},{96,128},{128,160},{160,192},{192,224},{224... | collective-permute-start | bytes 73736 | tf_op jit(solution)/shard_map/ppermute | solution.py:23
  366.6 7.9 %collective-permute-start.8 = (f32[6,8,1,128]{3,1,2,0:T(8,128)S(1)}, f32[6,8,1,128]{3,1,2,0:T(8,128)S(1)}, u32[]{:S(2)}, u32[]{:S(2)}) collective-permute-start(f32[6,8,1,128]{3,1,2,0:T(8,128)S(1)} %bitcast.290), channel_id=1, source_target_pairs={{32,0},{64,32},{96,64},{128,96},{160,128},{192,160},{224,192},{256... | collective-permute-start | bytes 73736 | tf_op jit(solution)/shard_map/ppermute | solution.py:24
  377.3 7.2 %collective-permute-start.11 = (f32[6,8,34,1]{2,1,3,0:T(8,128)}, f32[6,8,34,1]{2,1,3,0:T(8,128)S(1)}, u32[]{:S(2)}, u32[]{:S(2)}) collective-permute-start(f32[6,8,34,1]{2,1,3,0:T(8,128)} %copy.459), channel_id=1, source_target_pairs={{0,1},{1,2},{2,3},{3,4},{4,5},{5,6},{6,7},{7,8},{8,9},{9,10},{10,1... | collective-permute-start | bytes 19592 | tf_op jit(solution)/shard_map/ppermute | solution.py:23
  380.2 3.4 copy-start.51
  380.6 5.4 collective-permute-start.10
  387.3 1.9 copy-start.7
  387.3 2.0 copy-start.8
  387.3 2.0 copy-start.9
  390.3 29.4 %copy-start.1 = (f32[3,8,32,128]{3,2,1,0:T(8,128)}, f32[3,8,32,128]{3,2,1,0:T(8,128)S(1)}, u32[]{:S(2)}) copy-start(f32[3,8,32,128]{3,2,1,0:T(8,128)S(1)} %multiply_add_fusion) | copy-start | bytes 1179652
  390.3 9.5 %collective-permute-start.12 = (f32[3,8,1,128]{3,1,2,0:T(8,128)S(1)}, f32[3,8,1,128]{3,1,2,0:T(8,128)S(1)}, u32[]{:S(2)}, u32[]{:S(2)}) collective-permute-start(f32[3,8,1,128]{3,1,2,0:T(8,128)S(1)} %bitcast.295), channel_id=1, source_target_pairs={{32,0},{64,32},{96,64},{128,96},{160,128},{192,160},{224,192},{256... | collective-permute-start | bytes 36872 | tf_op jit(solution)/shard_map/ppermute | solution.py:24
  397.8 8.1 %collective-permute-start.13 = (f32[3,8,1,128]{3,1,2,0:T(8,128)S(1)}, f32[3,8,1,128]{3,1,2,0:T(8,128)S(1)}, u32[]{:S(2)}, u32[]{:S(2)}) collective-permute-start(f32[3,8,1,128]{3,1,2,0:T(8,128)S(1)} %bitcast.293), channel_id=1, source_target_pairs={{0,32},{32,64},{64,96},{96,128},{128,160},{160,192},{192,224},{224... | collective-permute-start | bytes 36872 | tf_op jit(solution)/shard_map/ppermute | solution.py:23
  406.2 8.8 %collective-permute-start.15 = (f32[3,8,34,1]{3,2,1,0:T(8,128)S(1)}, f32[3,8,34,1]{3,2,1,0:T(8,128)S(1)}, u32[]{:S(2)}, u32[]{:S(2)}) collective-permute-start(f32[3,8,34,1]{3,2,1,0:T(8,128)S(1)} %get-tuple-element.101), channel_id=1, source_target_pairs={{0,1},{1,2},{2,3},{3,4},{4,5},{5,6},{6,7},{7,8},{8,9},{9,10},{10,1... | collective-permute-start | bytes 9800 | tf_op jit(solution)/shard_map/ppermute | solution.py:23
  409.2 10.4 %collective-permute-start.14 = (f32[3,8,34,1]{3,2,1,0:T(8,128)S(1)}, f32[3,8,34,1]{3,2,1,0:T(8,128)S(1)}, u32[]{:S(2)}, u32[]{:S(2)}) collective-permute-start(f32[3,8,34,1]{3,2,1,0:T(8,128)S(1)} %get-tuple-element.100), channel_id=1, source_target_pairs={{1,0},{2,1},{3,2},{4,3},{5,4},{6,5},{7,6},{8,7},{9,8},{10,9},{11,1... | collective-permute-start | bytes 9800 | tf_op jit(solution)/shard_map/ppermute | solution.py:24
  414.3 5.8 %copy-start.6 = (f32[3,8,32,128]{3,2,1,0:T(8,128)S(1)}, f32[3,8,32,128]{3,2,1,0:T(8,128)}, u32[]{:S(2)}) copy-start(f32[3,8,32,128]{3,2,1,0:T(8,128)} %copy-done.5) | copy-start | bytes 1179652
  414.3 5.8 %copy-start.10 = (f32[8,32,128]{2,1,0:T(8,128)S(1)}, f32[8,32,128]{2,1,0:T(8,128)}, u32[]{:S(2)}) copy-start(f32[8,32,128]{2,1,0:T(8,128)} %get-tuple-element.61) | copy-start | bytes 393220
  420.3 1.0 copy-start.4
  421.5 127.7 %copy-start.50 = (f32[6,8,32,128]{3,2,1,0:T(8,128)}, f32[6,8,32,128]{3,2,1,0:T(8,128)S(1)}, u32[]{:S(2)}) copy-start(f32[6,8,32,128]{3,2,1,0:T(8,128)S(1)} %bitcast_dynamic-update-slice_fusion) | copy-start | bytes 2359300
  (24 other events, 18.7 us)
Sparse Core Ops, SparseCore 0:
  35.1 264.8 all-reduce.13
where the time goes:
time: 558 us; the launch traced here: 556 us
  waiting for transfers between devices  258 us (46%)
  blocking collectives  125 us (22%)
  starting transfers between devices  93.5 us (17%)
  other arithmetic  42.4 us (8%)
  local copies, waits for them, and re-layouts  20.8 us (4%)
  between operations  15.6 us (3%)
    psum x1, waiting for transfers between devices, broadcast(): return lax.psum(kept, axis)  227 us
    psum x1, blocking collectives, body(): shear = lax.psum(partial_shear, ('gx', 'gy'))  125 us
    ppermute x8, starting transfers between devices, with_halo(): after = lax.ppermute(leading, axis, down)  50.7 us
    ppermute x8, starting transfers between devices, with_halo(): before = lax.ppermute(last, axis, up)  42.7 us
    ppermute x8, waiting for transfers between devices, with_halo(): before = lax.ppermute(last, axis, up)  16.7 us
    ppermute x8, waiting for transfers between devices, with_halo(): after = lax.ppermute(leading, axis, down)  14.2 us
    unnamed x10, other arithmetic  12.5 us
  transfers between devices with their start and end apart: 17, of which 10 were waited for; matrix products, arithmetic and copies ran while one was open for 6% of the time, Pallas kernels for 0%

commit v1 on v0

v1 whole, which is shorter than its diff:
```python
import functools

import jax
import jax.numpy as jnp
from jax import lax
from jax.experimental import pallas as pl
from jax.experimental.pallas import tpu as pltpu
from jax.sharding import PartitionSpec as P

CX = 32
CY = 128
NZ = 8
STEPS = 2
COARSE = 4
BLOCK = 8
ZONES = 16
BUILDINGS = 1024
LANES = 128
PAD = 8
ROWS = 2 * BUILDINGS // LANES
MESH = pl.DeviceIdType.MESH
HIGH = lax.Precision.HIGHEST
F32 = jnp.float32

XX, XZ, XY, YY, YZ, ZZ = range(6)


def lane_of(shape):
    return lax.broadcasted_iota(jnp.int32, shape, len(shape) - 1)


def row_of(shape):
    return lax.broadcasted_iota(jnp.int32, shape, len(shape) - 2)


def kernel(
    owner, table, vel, stress_in, zones, regional, buildings, blocks,
    vel_out, stress_out, shear,
    S, V, lam, mu, buoy, drm, counts,
    xs, xr, ys, yr, reg_send, reg_recv, part, r1, q1, r2, q2, gathered,
    load_sem, store_sem, halo_send, halo_recv, reg_sems, sum_sems,
):
    GX, GY = lax.axis_size("gx"), lax.axis_size("gy")
    gx, gy = lax.axis_index("gx"), lax.axis_index("gy")
    nz_own = part.shape[0]

    core = pl.ds(PAD, CX)
    load_v = pltpu.make_async_copy(vel, V.at[:, :, core, :], load_sem.at[0])
    load_s = pltpu.make_async_copy(stress_in, S.at[:, :, core, :], load_sem.at[1])
    load_s.start()
    load_v.start()

    barrier = pltpu.get_barrier_semaphore()

    def greet_x(d, carry):
        pl.semaphore_signal(barrier, inc=1, device_id=((gx + d) % GX, gy), device_id_type=MESH)
        return carry

    def greet_y(d, carry):
        pl.semaphore_signal(barrier, inc=1, device_id=(gx, (gy + d) % GY), device_id_type=MESH)
        return carry

    lax.fori_loop(1, GX, greet_x, 0)
    lax.fori_loop(1, GY, greet_y, 0)

    def pack_regional(i, carry):
        for s in range(STEPS):
            for c in range(3):
                reg_send[i, s * 3 + c, 0:1, :] = regional[0, s, c, pl.ds(i, 1), :]
        return carry

    lax.fori_loop(0, GX, pack_regional, 0)

    lane = lane_of((CX, CY))
    first_lane = lane == 0
    last_lane = lane == CY - 1
    pair = lane >> 1
    odd = (lane & 1) == 1

    def exchange(r, ref, fx, fy, z0, z1):
        n = z1 - z0
        for k, f in enumerate(fx):
            xs[r, 0, k, 0:n, :] = ref[f, z0:z1, PAD, :]
            xs[r, 1, k, 0:n, :] = ref[f, z0:z1, PAD + CX - 1, :]
        acc = jnp.zeros((CX, CY), F32)
        m = 0
        for f in fy:
            for z in range(z0, z1):
                moved = pltpu.roll(ref[f, z, core, :], 2 * m + 1, 1)
                acc = jnp.where(pair == m, moved, acc)
                m += 1
        ys[r] = acc
        copies = []
        for d, (src, dst, to) in enumerate([
            (xs.at[r, 0], xr.at[r, 0], ((gx + GX - 1) % GX, gy)),
            (xs.at[r, 1], xr.at[r, 1], ((gx + 1) % GX, gy)),
            (ys.at[r], yr.at[r, 0], (gx, (gy + GY - 1) % GY)),
            (ys.at[r], yr.at[r, 1], (gx, (gy + 1) % GY)),
        ]):
            copy = pltpu.make_async_remote_copy(
                src_ref=src, dst_ref=dst, send_sem=halo_send.at[r, d],
                recv_sem=halo_recv.at[r, d], device_id=to, device_id_type=MESH)
            copies.append(copy)
        return copies

    def start(copies):
        for copy in copies:
            copy.start()

    def arrive(copies, r, ref, fx, z0, z1):
        n = z1 - z0
        for copy in copies:
            copy.wait_recv()
        for k, f in enumerate(fx):
            ref[f, z0:z1, PAD + CX, :] = xr[r, 0, k, 0:n, :]
            ref[f, z0:z1, PAD - 1, :] = xr[r, 1, k, 0:n, :]
        from_right = pltpu.roll(yr[r, 0], CY - 1, 1)
        from_left = pltpu.roll(yr[r, 1], 1, 1)
        return jnp.where(odd, from_left, from_right)

    def diff_x(ref, f, z):
        return ref[f, z, pl.ds(PAD + 1, CX), :] - ref[f, z, pl.ds(PAD - 1, CX), :]

    def diff_y(ref, f, z, edge, m):
        value = ref[f, z, core, :]
        moved = pltpu.roll(edge, CY - (2 * m + 1), 1)
        after = jnp.where(last_lane, moved, pltpu.roll(value, CY - 1, 1))
        before = jnp.where(first_lane, moved, pltpu.roll(value, 1, 1))
        return after - before

    def diff_z(ref, f, z):
        if z == 0:
            return ref[f, 1, core, :]
        if z == NZ - 1:
            return -ref[f, NZ - 2, core, :]
        return ref[f, z + 1, core, :] - ref[f, z - 1, core, :]

    def velocity_planes(step, edge, e0, e1, z0, z1):
        ne = e1 - e0
        for z in range(z0, z1):
            k = z - e0
            b = buoy[z]
            force = [
                diff_x(S, XX, z) + diff_y(S, XY, z, edge, k) + diff_z(S, XZ, z),
                diff_x(S, XY, z) + diff_y(S, YY, z, edge, ne + k) + diff_z(S, YZ, z),
                diff_x(S, XZ, z) + diff_y(S, YZ, z, edge, 2 * ne + k) + diff_z(S, ZZ, z),
            ]
            for c in range(3):
                f = force[c]
                if z == NZ - 1:
                    f = f + 20.0 * mu[z] * drm[step * 3 + c]
                V[c, z, core, :] = V[c, z, core, :] + b * f

    def stress_planes(edge, e0, e1, z0, z1):
        ne = e1 - e0
        for z in range(z0, z1):
            k = z - e0
            m1 = mu[z]
            dvx = diff_x(V, 0, z)
            dvy = diff_y(V, 1, z, edge, ne + k)
            dvz = diff_z(V, 2, z)
            common = lam[z] * (dvx + dvy + dvz)
            m2 = m1 + m1
            S[XX, z, core, :] = S[XX, z, core, :] + (common + m2 * dvx)
            S[YY, z, core, :] = S[YY, z, core, :] + (common + m2 * dvy)
            S[ZZ, z, core, :] = S[ZZ, z, core, :] + (common + m2 * dvz)
            S[XZ, z, core, :] = S[XZ, z, core, :] + m1 * (diff_z(V, 0, z) + diff_x(V, 2, z))
            S[XY, z, core, :] = S[XY, z, core, :] + m1 * (diff_y(V, 0, z, edge, k) + diff_x(V, 1, z))
            S[YZ, z, core, :] = S[YZ, z, core, :] + m1 * (diff_z(V, 1, z) + diff_y(V, 2, z, edge, 2 * ne + k))

    SX, SY, VX, VY = (XX, XY, XZ), (XY, YY, YZ), (0, 1, 2), (0, 1, 2)

    load_s.wait()
    c0 = exchange(0, S, SX, SY, 0, NZ)
    pl.semaphore_wait(barrier, GX + GY - 2)
    start(c0)

    reg_slot = gx

    def send_regional(d, carry):
        to = (gx + d) % GX
        pltpu.make_async_remote_copy(
            src_ref=reg_send.at[to], dst_ref=reg_recv.at[reg_slot], send_sem=reg_sems.at[0],
            recv_sem=reg_sems.at[1], device_id=(to, gy), device_id_type=MESH).start()
        return carry

    lax.fori_loop(1, GX, send_regional, 0)
    reg_recv[reg_slot] = reg_send[gx]

    for z in range(NZ):
        zone = zones[z]
        bits = [(zone & (1 << b)) != 0 for b in range(4)]
        for row, target in ((0, lam), (1, mu), (2, buoy)):
            level = [table[row, t] * 0.1 for t in range(ZONES)]
            for b in range(4):
                level = [
                    jnp.where(bits[b], level[2 * t + 1], level[2 * t]) for t in range(len(level) // 2)
                ]
            target[z] = level[0]

    n_blocks = (CX // BLOCK) * (CY // BLOCK)
    entries = blocks.shape[-1]
    block_hot = (blocks[0] == row_of((n_blocks, entries))).astype(jnp.bfloat16)
    building_hot = (buildings[0] == row_of((BUILDINGS, entries))).astype(jnp.bfloat16)
    counts[...] = lax.dot_general(
        block_hot, building_hot, (((1,), (1,)), ((), ())), preferred_element_type=F32)

    load_v.wait()

    def whole(src, dst, send_sem, recv_sem):
        return pltpu.make_async_remote_copy(
            src_ref=src, dst_ref=dst, send_sem=send_sem, recv_sem=recv_sem,
            device_id=((gx + 1) % GX, gy), device_id_type=MESH)

    all_regional = whole(
        reg_send.at[pl.ds(0, GX - 1)], reg_recv.at[pl.ds(0, GX - 1)], reg_sems.at[0], reg_sems.at[1])

    def take_regional():
        all_regional.wait_recv()
        root = owner[gy]
        wide = (CX, 2 * LANES)
        mine = reg_recv[root]
        keep = (lane_of(wide) >> 5) == (row_of(wide) >> 2)
        rows = jnp.concatenate(
            [jnp.where(keep, jnp.broadcast_to(mine[q], wide), 0.0) for q in range(6)], axis=0)
        spread_shape = (2 * LANES, CY)
        spread = ((row_of(spread_shape) & 31) == (lane_of(spread_shape) >> 2)).astype(F32)
        plane = jnp.dot(rows, spread, precision=HIGH, preferred_element_type=F32)
        for q in range(6):
            drm[q] = plane[q * CX:(q + 1) * CX, :]

    started = []

    def round_trip(r, ref, fx, fy, z0, z1):
        copies = exchange(r, ref, fx, fy, z0, z1)
        start(copies)
        started.append(copies)
        return copies

    started.append(c0)

    e0 = arrive(c0, 0, S, SX, 0, NZ)
    velocity_planes(0, e0, 0, NZ, 0, 5)
    c = round_trip(1, V, VX, VY, 0, 5)
    e1 = arrive(c, 1, V, VX, 0, 5)
    velocity_rest = (5, NZ)
    take_regional()
    velocity_planes(0, e0, 0, NZ, *velocity_rest)
    c_b1 = round_trip(2, V, VX, VY, 5, NZ)
    stress_planes(e1, 0, 5, 0, 4)
    c = round_trip(3, S, SX, SY, 0, 4)
    e2 = arrive(c, 3, S, SX, 0, 4)
    eb1 = arrive(c_b1, 2, V, VX, 5, NZ)
    stress_planes(e1, 0, 5, 4, 5)
    stress_planes(eb1, 5, NZ, 5, NZ)
    c_b2 = round_trip(4, S, SX, SY, 4, NZ)
    velocity_planes(1, e2, 0, 4, 0, 3)
    c = round_trip(5, V, VX, VY, 0, 3)
    e3 = arrive(c, 5, V, VX, 0, 3)
    eb2 = arrive(c_b2, 4, S, SX, 4, NZ)
    velocity_planes(1, e2, 0, 4, 3, 4)
    velocity_planes(1, eb2, 4, NZ, 4, NZ)
    c_b3 = round_trip(6, V, VX, VY, 3, NZ)
    save_v = pltpu.make_async_copy(V.at[:, :, core, :], vel_out, store_sem.at[0])
    save_v.start()
    stress_planes(e3, 0, 3, 0, 3)

    sums = jnp.concatenate(
        [jnp.sum(S[f, 1, core, :].reshape(CX // BLOCK, BLOCK, CY), axis=1) for f in (XZ, YZ)], axis=0)
    fold_shape = (CY, n_blocks)
    fold = ((row_of(fold_shape) >> 3) == (lane_of(fold_shape) & 15)).astype(F32)
    per_block = jnp.dot(sums, fold, precision=HIGH, preferred_element_type=F32)
    mask_shape = (8, n_blocks)
    own_row = (row_of(mask_shape) & 3) == (lane_of(mask_shape) >> 4)
    per_block = jnp.where(own_row, per_block, 0.0) * (1.0 / (BLOCK * BLOCK))
    total = jnp.dot(per_block, counts[...], precision=HIGH, preferred_element_type=F32)
    per_owner = ROWS // nz_own
    for comp in range(2):
        row = jnp.sum(total[4 * comp:4 * comp + 4], axis=0, keepdims=True)
        for t in range(BUILDINGS // LANES):
            k = comp * (BUILDINGS // LANES) + t
            part[k // per_owner, k % per_owner] = row[:, t * LANES:(t + 1) * LANES]

    mine_row = gx % nz_own

    def send_part(d, carry):
        to = (gx + d) % GX
        pltpu.make_async_remote_copy(
            src_ref=part.at[to % nz_own], dst_ref=r1.at[gx], send_sem=sum_sems.at[0],
            recv_sem=sum_sems.at[1], device_id=(to, gy), device_id_type=MESH).start()
        return carry

    lax.fori_loop(1, GX, send_part, 0)
    r1[gx] = part[mine_row]
    wait_r1 = whole(r1.at[pl.ds(0, GX - 1)], r1.at[pl.ds(0, GX - 1)], sum_sems.at[0], sum_sems.at[1])
    wait_r1.wait_recv()
    q1[...] = jnp.sum(r1[...], axis=0)

    def send_row(d, carry):
        to = (gy + d) % GY
        pltpu.make_async_remote_copy(
            src_ref=q1, dst_ref=r2.at[gy], send_sem=sum_sems.at[2],
            recv_sem=sum_sems.at[3], device_id=(gx, to), device_id_type=MESH).start()
        return carry

    lax.fori_loop(1, GY, send_row, 0)
    r2[gy] = q1[...]
    wait_r2 = whole(r2.at[pl.ds(0, GY - 1)], r2.at[pl.ds(0, GY - 1)], sum_sems.at[2], sum_sems.at[3])

    eb3 = arrive(c_b3, 6, V, VX, 3, NZ)
    stress_planes(eb3, 3, NZ, 3, NZ)
    save_s = pltpu.make_async_copy(S.at[:, :, core, :], stress_out, store_sem.at[1])
    save_s.start()

    wait_r2.wait_recv()
    q2[...] = jnp.sum(r2[...], axis=0)

    base = gx - mine_row

    def send_total(d, carry):
        to = base + (mine_row + d) % nz_own
        pltpu.make_async_remote_copy(
            src_ref=q2, dst_ref=gathered.at[mine_row], send_sem=sum_sems.at[4],
            recv_sem=sum_sems.at[5], device_id=(to, gy), device_id_type=MESH).start()
        return carry

    lax.fori_loop(1, nz_own, send_total, 0)
    gathered[mine_row] = q2[...]
    some = pl.ds(0, nz_own - 1)
    wait_g = whole(gathered.at[some], gathered.at[some], sum_sems.at[4], sum_sems.at[5])
    wait_g.wait_recv()
    for comp in range(2):
        for t in range(BUILDINGS // LANES):
            k = comp * (BUILDINGS // LANES) + t
            shear[comp:comp + 1, t * LANES:(t + 1) * LANES] = gathered[k // per_owner, k % per_owner]

    for copies in started:
        for copy in copies:
            copy.wait_send()
    all_regional.wait_send()
    wait_r1.wait_send()
    wait_r2.wait_send()
    wait_g.wait_send()
    save_v.wait()
    save_s.wait()


def body(velocity, stress, zones, zone_table, regional, owner, footprint_building, footprint_block):
    GX, GY = lax.axis_size("gx"), lax.axis_size("gy")
    nz_own = min(GX, ROWS)
    per_owner = ROWS // nz_own
    rounds = 7
    vmem = pl.BlockSpec(memory_space=pltpu.VMEM)
    smem = pl.BlockSpec(memory_space=pltpu.SMEM)
    hbm = pl.BlockSpec(memory_space=pl.ANY)
    dma = pltpu.SemaphoreType.DMA
    return pl.pallas_call(
        kernel,
        out_shape=(
            jax.ShapeDtypeStruct(velocity.shape, F32),
            jax.ShapeDtypeStruct(stress.shape, F32),
            jax.ShapeDtypeStruct((2, BUILDINGS), F32),
        ),
        in_specs=[smem, smem, hbm, hbm, vmem, vmem, vmem, vmem],
        out_specs=(hbm, hbm, vmem),
        scratch_shapes=[
            pltpu.VMEM((6, NZ, CX + 2 * PAD, CY), F32),
            pltpu.VMEM((3, NZ, CX + 2 * PAD, CY), F32),
            pltpu.VMEM((NZ, CX, CY), F32),
            pltpu.VMEM((NZ, CX, CY), F32),
            pltpu.VMEM((NZ, CX, CY), F32),
            pltpu.VMEM((6, CX, CY), F32),
            pltpu.VMEM((64, BUILDINGS), F32),
            pltpu.VMEM((rounds, 2, 3, NZ, CY), F32),
            pltpu.VMEM((rounds, 2, 3, NZ, CY), F32),
            pltpu.VMEM((rounds, CX, CY), F32),
            pltpu.VMEM((rounds, 2, CX, CY), F32),
            pltpu.VMEM((GX, 6, 1, 2 * LANES), F32),
            pltpu.VMEM((GX, 6, 1, 2 * LANES), F32),
            pltpu.VMEM((nz_own, per_owner, 1, LANES), F32),
            pltpu.VMEM((GX, per_owner, 1, LANES), F32),
            pltpu.VMEM((per_owner, 1, LANES), F32),
            pltpu.VMEM((GY, per_owner, 1, LANES), F32),
            pltpu.VMEM((per_owner, 1, LANES), F32),
            pltpu.VMEM((nz_own, per_owner, 1, LANES), F32),
            dma((2,)),
            dma((2,)),
            dma((rounds, 4)),
            dma((rounds, 4)),
            dma((2,)),
            dma((6,)),
        ],
        compiler_params=pltpu.CompilerParams(
            collective_id=0, has_side_effects=True, vmem_limit_bytes=32 * 1024 * 1024
        ),
    )(owner, zone_table, velocity, stress, zones, regional, footprint_building, footprint_block)


def solution(mesh):
    return jax.shard_map(
        body,
        mesh=mesh,
        in_specs=(
            P(None, None, "gx", "gy"),
            P(None, None, "gx", "gy"),
            P(None, "gx", "gy"),
            P(),
            P("gx", None, None, None, "gy"),
            P(),
            P("gx", "gy", None),
            P("gx", "gy", None),
        ),
        out_specs=(P(None, None, "gx", "gy"), P(None, None, "gx", "gy"), P()),
        check_vma=False,
    )
```

time: 558 us -> 81.8 us (0.15)
  waiting for transfers between devices: 258 us -> 0 us
  blocking collectives: 125 us -> 0 us
  starting transfers between devices: 93.5 us -> 0 us
  Pallas kernels: 0 us -> 72 us
  other arithmetic: 42.4 us -> 0 us
  between operations: 15.6 us -> 0.66 us
  local copies, waits for them, and re-layouts: 20.8 us -> 8.82 us
    psum x1 -> x0, waiting for transfers between devices: 227 us -> none  [broadcast(): return lax.psum(kept, axis)]
    psum x1 -> x0, blocking collectives: 125 us -> none  [body(): shear = lax.psum(partial_shear, ('gx', 'gy'))]
    ppermute x16 -> x0, starting transfers between devices: 93.4 us -> none  [the longest x8 50.7 us: with_halo(): after = lax.ppermute(leading, axis, down)]
    pallas_call x0 -> x1, Pallas kernels: none -> 72 us  [body(): pl.pallas_call(kernel, out_shape=(jax.ShapeDtypeStruct(velocity.shape, F3...]
    ppermute x16 -> x0, waiting for transfers between devices: 30.9 us -> none  [the longest x8 16.7 us: with_halo(): before = lax.ppermute(last, axis, up)]
    mul x6 -> x0, other arithmetic: 14.5 us -> none  [the longest x1 10.3 us: body(): velocity = velocity + 0.2 * buoy[None] * force]
    unnamed x10 -> x0, other arithmetic: 12.5 us -> none
    add x3 -> x0, other arithmetic: 10.7 us -> none  [the longest x1 10.5 us: lookup(): total = total + jnp.where(zones == zone, column[zone], 0.0)]
  transfers between devices with their start and end apart: 17 -> 0, of which waited for: 10 -> 0; matrix products, arithmetic and copies ran while one was open for 6% -> 0% of each run, Pallas kernels for 0% -> 0%
where the time goes in v1:
time: 81.8 us; the launch traced here: 81.4 us
  Pallas kernels  72 us (88%)
  local copies, waits for them, and re-layouts  8.82 us (11%)
    pallas_call x1, Pallas kernels, body(): pl.pallas_call(kernel, out_shape=(jax.ShapeDtypeStruct(velocity.shape, F3...  72 us
    unnamed x19, local copies, waits for them, and re-layouts  8.82 us

profile of v1, /device:TPU:1, one launch (start us, length us, event | category | flops | bytes accessed | tf_op | source)
XLA Modules:
  0.0 81.4 jit_solution(1290277408863823719)
XLA Ops:
  0.6 0.0 copy-start
  0.6 1.1 %copy-done = f32[6,8,32,128]{3,2,1,0:T(8,128)S(1)} copy-done((f32[6,8,32,128]{3,2,1,0:T(8,128)S(1)}, f32[6,8,32,128]{3,2,1,0:T(8,128)}, u32[]{:S(2)}) %copy-start) | copy-done | bytes 786456
  1.8 0.0 copy-start.1
  1.8 1.0 %copy-done.1 = f32[3,8,32,128]{3,2,1,0:T(8,128)S(1)} copy-done((f32[3,8,32,128]{3,2,1,0:T(8,128)S(1)}, f32[3,8,32,128]{3,2,1,0:T(8,128)}, u32[]{:S(2)}) %copy-start.1) | copy-done | bytes 393240
  2.8 0.0 copy-start.2
  2.8 0.9 %copy-done.2 = f32[1,2,3,32,256]{4,3,2,1,0:T(8,128)S(1)} copy-done((f32[1,2,3,32,256]{4,3,2,1,0:T(8,128)S(1)}, f32[1,2,3,32,256]{4,3,2,1,0:T(8,128)}, u32[]{:S(2)}) %copy-start.2) | copy-done | bytes 196632
  3.7 0.0 copy-start.3
  3.7 0.9 %copy-done.3 = s32[8,32,128]{2,1,0:T(8,128)S(1)} copy-done((s32[8,32,128]{2,1,0:T(8,128)S(1)}, s32[8,32,128]{2,1,0:T(8,128)}, u32[]{:S(2)}) %copy-start.3) | copy-done | bytes 131096
  4.6 0.0 copy-start.4
  4.6 0.7 copy-done.4
  5.3 0.0 copy-start.5
  5.3 0.7 copy-done.5
  5.9 0.0 copy-start.6
  5.9 0.7 copy-done.6
  6.6 0.0 copy-start.7
  6.6 0.7 copy-done.7
  7.2 72.0 %shard_map.103 = (f32[3,8,32,128]{3,2,1,0:T(8,128)S(1)}, f32[6,8,32,128]{3,2,1,0:T(8,128)S(1)}, f32[2,1024]{1,0:T(2,128)S(1)}) custom-call(s32[32]{0:T(128)S(1)} %copy-done.5, f32[3,16]{1,0:T(4,128)S(1)} %copy-done.4, f32[3,8,32,128]{3,2,1,0:T(8,128)S(1)} %copy-done.1, f32[6,8,32,128]{3,2,1,0:T(8,128)S(1)} %copy-done, s32[8,32,128]{2,1,0:T(8,128)S(1)} %copy-done.3, ...), custom_call_target="tpu_custom_call" | custom-call | tf_op jit(solution)/shard_map/pallas_call | solution.py:357
  79.2 0.7 copy.14
  80.0 0.9 %copy.15 = f32[6,8,32,128]{3,2,1,0:T(8,128)} copy(f32[6,8,32,128]{3,2,1,0:T(8,128)S(1)} %get-tuple-element.7) | data formatting | bytes 1572864
  80.8 0.6 copy.16
Async XLA Ops:
  0.6 1.1 %copy-start = (f32[6,8,32,128]{3,2,1,0:T(8,128)S(1)}, f32[6,8,32,128]{3,2,1,0:T(8,128)}, u32[]{:S(2)}) copy-start(f32[6,8,32,128]{3,2,1,0:T(8,128)} %stress_in.1) | copy-start | bytes 2359300
  1.8 1.0 %copy-start.1 = (f32[3,8,32,128]{3,2,1,0:T(8,128)S(1)}, f32[3,8,32,128]{3,2,1,0:T(8,128)}, u32[]{:S(2)}) copy-start(f32[3,8,32,128]{3,2,1,0:T(8,128)} %vel.1) | copy-start | bytes 1179652
  2.8 0.9 %copy-start.2 = (f32[1,2,3,32,256]{4,3,2,1,0:T(8,128)S(1)}, f32[1,2,3,32,256]{4,3,2,1,0:T(8,128)}, u32[]{:S(2)}) copy-start(f32[1,2,3,32,256]{4,3,2,1,0:T(8,128)} %regional.1) | copy-start | bytes 589828
  3.7 0.9 %copy-start.3 = (s32[8,32,128]{2,1,0:T(8,128)S(1)}, s32[8,32,128]{2,1,0:T(8,128)}, u32[]{:S(2)}) copy-start(s32[8,32,128]{2,1,0:T(8,128)} %zones.1) | copy-start | bytes 393220
  4.6 0.7 copy-start.4
  5.3 0.7 copy-start.5
  5.9 0.7 copy-start.6
  6.6 0.7 copy-start.7

commit v2 on v1

--- a/solution.py
+++ b/solution.py
@@ -33,43 +33,57 @@
     return lax.broadcasted_iota(jnp.int32, shape, len(shape) - 2)
 
 
+def layers(gx_size):
+    z_size = min(gx_size, 16)
+    return z_size, gx_size // z_size
+
+
 def kernel(
-    owner, table, vel, stress_in, zones, regional, buildings, blocks,
+    owner_hbm, table_hbm, vel, stress_in, zones_hbm, regional_hbm, buildings_hbm, blocks_hbm,
     vel_out, stress_out, shear,
     S, V, lam, mu, buoy, drm, counts,
-    xs, xr, ys, yr, reg_send, reg_recv, part, r1, q1, r2, q2, gathered,
-    load_sem, store_sem, halo_send, halo_recv, reg_sems, sum_sems,
+    xs, xr, ys, yr, reg_send, reg_recv, part, r1, q1, hub, q2, gathered,
+    owner, table, zones, regional, buildings, blocks,
+    load_sem, store_sem, halo_send, halo_recv, reg_sems, sum_sems, entered, beside,
 ):
     GX, GY = lax.axis_size("gx"), lax.axis_size("gy")
     gx, gy = lax.axis_index("gx"), lax.axis_index("gy")
-    nz_own = part.shape[0]
+    z_size, x_size = layers(GX)
+    owners = part.shape[0]
+    z_me = gx % z_size
+    base_x = gx - z_me
+
+    def rank_of(g):
+        return (g % z_size) * x_size + g // z_size
+
+    def at_rank(q):
+        return (q % x_size) * z_size + q // x_size
+
+    me = rank_of(gx)
 
     core = pl.ds(PAD, CX)
-    load_v = pltpu.make_async_copy(vel, V.at[:, :, core, :], load_sem.at[0])
-    load_s = pltpu.make_async_copy(stress_in, S.at[:, :, core, :], load_sem.at[1])
-    load_s.start()
-    load_v.start()
+    loads = [
+        pltpu.make_async_copy(src, dst, load_sem.at[k]) for k, (src, dst) in enumerate([
+            (stress_in, S.at[:, :, core, :]), (vel, V.at[:, :, core, :]), (regional_hbm, regional),
+            (zones_hbm, zones), (table_hbm, table), (owner_hbm, owner), (buildings_hbm, buildings),
+            (blocks_hbm, blocks),
+        ])
+    ]
+    for load in loads:
+        load.start()
 
     barrier = pltpu.get_barrier_semaphore()
 
-    def greet_x(d, carry):
-        pl.semaphore_signal(barrier, inc=1, device_id=((gx + d) % GX, gy), device_id_type=MESH)
+    def greet_x(q, carry):
+        pl.semaphore_signal(barrier, inc=1, device_id=(at_rank(q), gy), device_id_type=MESH)
         return carry
 
     def greet_y(d, carry):
         pl.semaphore_signal(barrier, inc=1, device_id=(gx, (gy + d) % GY), device_id_type=MESH)
         return carry
 
-    lax.fori_loop(1, GX, greet_x, 0)
     lax.fori_loop(1, GY, greet_y, 0)
-
-    def pack_regional(i, carry):
-        for s in range(STEPS):
-            for c in range(3):
-                reg_send[i, s * 3 + c, 0:1, :] = regional[0, s, c, pl.ds(i, 1), :]
-        return carry
-
-    lax.fori_loop(0, GX, pack_regional, 0)
+    lax.fori_loop(me + 1, GX, greet_x, 0)
 
     lane = lane_of((CX, CY))
     first_lane = lane == 0
@@ -170,22 +184,79 @@
 
     SX, SY, VX, VY = (XX, XY, XZ), (XY, YY, YZ), (0, 1, 2), (0, 1, 2)
 
-    load_s.wait()
+    loads[0].wait()
     c0 = exchange(0, S, SX, SY, 0, NZ)
-    pl.semaphore_wait(barrier, GX + GY - 2)
-    start(c0)
-
-    reg_slot = gx
-
-    def send_regional(d, carry):
-        to = (gx + d) % GX
+    pl.semaphore_wait(barrier, me + GY - 1)
+
+    after, before = (gx + 1) % GX, (gx + GX - 1) % GX
+
+    @pl.when(rank_of(after) < me)
+    def _():
+        pl.semaphore_signal(beside.at[1], inc=1, device_id=(after, gy), device_id_type=MESH)
+
+    @pl.when(rank_of(before) < me)
+    def _():
+        pl.semaphore_signal(beside.at[0], inc=1, device_id=(before, gy), device_id_type=MESH)
+
+    @pl.when(rank_of(before) < me)
+    def _():
+        c0[0].start()
+
+    @pl.when(rank_of(after) < me)
+    def _():
+        c0[1].start()
+
+    c0[2].start()
+    c0[3].start()
+
+    def answer(q, carry):
+        pl.semaphore_signal(entered.at[me], inc=1, device_id=(at_rank(q), gy), device_id_type=MESH)
+        return carry
+
+    lax.fori_loop(0, me, answer, 0)
+
+    loads[2].wait()
+
+    def pack_regional(i, carry):
+        for s in range(STEPS):
+            for c in range(3):
+                reg_send[i, s * 3 + c, 0:1, :] = regional[0, s, c, pl.ds(i, 1), :]
+        return carry
+
+    lax.fori_loop(0, GX, pack_regional, 0)
+
+    def send_regional(q):
+        to = at_rank(q)
         pltpu.make_async_remote_copy(
-            src_ref=reg_send.at[to], dst_ref=reg_recv.at[reg_slot], send_sem=reg_sems.at[0],
+            src_ref=reg_send.at[to], dst_ref=reg_recv.at[gx], send_sem=reg_sems.at[0],
             recv_sem=reg_sems.at[1], device_id=(to, gy), device_id_type=MESH).start()
-        return carry
-
-    lax.fori_loop(1, GX, send_regional, 0)
-    reg_recv[reg_slot] = reg_send[gx]
+
+    def send_lower(q, carry):
+        send_regional(q)
+        return carry
+
+    def send_higher(q, carry):
+        pl.semaphore_wait(entered.at[q], 1)
+        send_regional(q)
+        return carry
+
+    lax.fori_loop(0, me, send_lower, 0)
+    reg_recv[gx] = reg_send[gx]
+    near = jnp.minimum(me + 1 + 3 * x_size, GX)
+    middle = jnp.minimum(me + 1 + 5 * x_size, GX)
+
+    @pl.when(rank_of(before) > me)
+    def _():
+        pl.semaphore_wait(beside.at[1], 1)
+        c0[0].start()
+
+    @pl.when(rank_of(after) > me)
+    def _():
+        pl.semaphore_wait(beside.at[0], 1)
+        c0[1].start()
+
+    for k in (3, 4, 6, 7):
+        loads[k].wait()
 
     for z in range(NZ):
         zone = zones[z]
@@ -205,7 +276,9 @@
     counts[...] = lax.dot_general(
         block_hot, building_hot, (((1,), (1,)), ((), ())), preferred_element_type=F32)
 
-    load_v.wait()
+    loads[1].wait()
+    loads[5].wait()
+    lax.fori_loop(me + 1, near, send_higher, 0)
 
     def whole(src, dst, send_sem, recv_sem):
         return pltpu.make_async_remote_copy(
@@ -242,28 +315,15 @@
     e0 = arrive(c0, 0, S, SX, 0, NZ)
     velocity_planes(0, e0, 0, NZ, 0, 5)
     c = round_trip(1, V, VX, VY, 0, 5)
+    lax.fori_loop(near, middle, send_higher, 0)
     e1 = arrive(c, 1, V, VX, 0, 5)
-    velocity_rest = (5, NZ)
-    take_regional()
-    velocity_planes(0, e0, 0, NZ, *velocity_rest)
-    c_b1 = round_trip(2, V, VX, VY, 5, NZ)
     stress_planes(e1, 0, 5, 0, 4)
     c = round_trip(3, S, SX, SY, 0, 4)
     e2 = arrive(c, 3, S, SX, 0, 4)
-    eb1 = arrive(c_b1, 2, V, VX, 5, NZ)
-    stress_planes(e1, 0, 5, 4, 5)
-    stress_planes(eb1, 5, NZ, 5, NZ)
-    c_b2 = round_trip(4, S, SX, SY, 4, NZ)
     velocity_planes(1, e2, 0, 4, 0, 3)
     c = round_trip(5, V, VX, VY, 0, 3)
     e3 = arrive(c, 5, V, VX, 0, 3)
-    eb2 = arrive(c_b2, 4, S, SX, 4, NZ)
-    velocity_planes(1, e2, 0, 4, 3, 4)
-    velocity_planes(1, eb2, 4, NZ, 4, NZ)
-    c_b3 = round_trip(6, V, VX, VY, 3, NZ)
-    save_v = pltpu.make_async_copy(V.at[:, :, core, :], vel_out, store_sem.at[0])
-    save_v.start()
-    stress_planes(e3, 0, 3, 0, 3)
+    stress_planes(e3, 0, 3, 0, 2)
 
     sums = jnp.concatenate(
         [jnp.sum(S[f, 1, core, :].reshape(CX // BLOCK, BLOCK, CY), axis=1) for f in (XZ, YZ)], axis=0)
@@ -274,72 +334,118 @@
     own_row = (row_of(mask_shape) & 3) == (lane_of(mask_shape) >> 4)
     per_block = jnp.where(own_row, per_block, 0.0) * (1.0 / (BLOCK * BLOCK))
     total = jnp.dot(per_block, counts[...], precision=HIGH, preferred_element_type=F32)
-    per_owner = ROWS // nz_own
+    per_owner = ROWS // owners
     for comp in range(2):
         row = jnp.sum(total[4 * comp:4 * comp + 4], axis=0, keepdims=True)
         for t in range(BUILDINGS // LANES):
             k = comp * (BUILDINGS // LANES) + t
             part[k // per_owner, k % per_owner] = row[:, t * LANES:(t + 1) * LANES]
 
-    mine_row = gx % nz_own
+    my_row = gy % owners
 
     def send_part(d, carry):
-        to = (gx + d) % GX
+        to = (gy + d) % GY
         pltpu.make_async_remote_copy(
-            src_ref=part.at[to % nz_own], dst_ref=r1.at[gx], send_sem=sum_sems.at[0],
-            recv_sem=sum_sems.at[1], device_id=(to, gy), device_id_type=MESH).start()
-        return carry
-
-    lax.fori_loop(1, GX, send_part, 0)
-    r1[gx] = part[mine_row]
-    wait_r1 = whole(r1.at[pl.ds(0, GX - 1)], r1.at[pl.ds(0, GX - 1)], sum_sems.at[0], sum_sems.at[1])
+            src_ref=part.at[to % owners], dst_ref=r1.at[gy], send_sem=sum_sems.at[0],
+            recv_sem=sum_sems.at[1], device_id=(gx, to), device_id_type=MESH).start()
+        return carry
+
+    lax.fori_loop(1, GY, send_part, 0)
+    r1[gy] = part[my_row]
+    lax.fori_loop(middle, GX, send_higher, 0)
+    peers_y = pl.ds(0, GY - 1)
+    wait_r1 = whole(r1.at[peers_y], r1.at[peers_y], sum_sems.at[0], sum_sems.at[1])
     wait_r1.wait_recv()
     q1[...] = jnp.sum(r1[...], axis=0)
 
-    def send_row(d, carry):
-        to = (gy + d) % GY
+    is_hub = z_me == 0
+    for x in range(x_size):
+        @pl.when(gx != x * z_size)
+        def _():
+            pltpu.make_async_remote_copy(
+                src_ref=q1, dst_ref=hub.at[gx], send_sem=sum_sems.at[2],
+                recv_sem=sum_sems.at[3], device_id=(x * z_size, gy), device_id_type=MESH).start()
+
+    take_regional()
+    velocity_planes(0, e0, 0, NZ, 5, NZ)
+    c = round_trip(2, V, VX, VY, 5, NZ)
+    eb1 = arrive(c, 2, V, VX, 5, NZ)
+    stress_planes(e1, 0, 5, 4, 5)
+    stress_planes(eb1, 5, NZ, 5, NZ)
+    c = round_trip(4, S, SX, SY, 4, NZ)
+
+    peers_x = pl.ds(0, GX - 1)
+    wait_hub = whole(hub.at[peers_x], hub.at[peers_x], sum_sems.at[2], sum_sems.at[3])
+
+    def send_down(z, carry):
         pltpu.make_async_remote_copy(
-            src_ref=q1, dst_ref=r2.at[gy], send_sem=sum_sems.at[2],
-            recv_sem=sum_sems.at[3], device_id=(gx, to), device_id_type=MESH).start()
-        return carry
-
-    lax.fori_loop(1, GY, send_row, 0)
-    r2[gy] = q1[...]
-    wait_r2 = whole(r2.at[pl.ds(0, GY - 1)], r2.at[pl.ds(0, GY - 1)], sum_sems.at[2], sum_sems.at[3])
-
-    eb3 = arrive(c_b3, 6, V, VX, 3, NZ)
-    stress_planes(eb3, 3, NZ, 3, NZ)
-    save_s = pltpu.make_async_copy(S.at[:, :, core, :], stress_out, store_sem.at[1])
-    save_s.start()
-
-    wait_r2.wait_recv()
-    q2[...] = jnp.sum(r2[...], axis=0)
-
-    base = gx - mine_row
+            src_ref=q2, dst_ref=q2, send_sem=sum_sems.at[4],
+            recv_sem=sum_sems.at[5], device_id=(base_x + z, gy), device_id_type=MESH).start()
+        return carry
+
+    down = whole(q2, q2, sum_sems.at[4], sum_sems.at[5])
+
+    @pl.when(is_hub)
+    def _():
+        hub[gx] = q1[...]
+        wait_hub.wait_recv()
+        q2[...] = jnp.sum(hub[...], axis=0)
+        lax.fori_loop(1, z_size, send_down, 0)
+
+    @pl.when(z_me != 0)
+    def _():
+        down.wait_recv()
+
+    base = gy - my_row
 
     def send_total(d, carry):
-        to = base + (mine_row + d) % nz_own
+        to = base + (my_row + d) % owners
         pltpu.make_async_remote_copy(
-            src_ref=q2, dst_ref=gathered.at[mine_row], send_sem=sum_sems.at[4],
-            recv_sem=sum_sems.at[5], device_id=(to, gy), device_id_type=MESH).start()
-        return carry
-
-    lax.fori_loop(1, nz_own, send_total, 0)
-    gathered[mine_row] = q2[...]
-    some = pl.ds(0, nz_own - 1)
-    wait_g = whole(gathered.at[some], gathered.at[some], sum_sems.at[4], sum_sems.at[5])
+            src_ref=q2, dst_ref=gathered.at[my_row], send_sem=sum_sems.at[6],
+            recv_sem=sum_sems.at[7], device_id=(gx, to), device_id_type=MESH).start()
+        return carry
+
+    lax.fori_loop(1, owners, send_total, 0)
+    gathered[my_row] = q2[...]
+
+    eb2 = arrive(c, 4, S, SX, 4, NZ)
+    velocity_planes(1, e2, 0, 4, 3, 4)
+    velocity_planes(1, eb2, 4, NZ, 4, NZ)
+    c = round_trip(6, V, VX, VY, 3, NZ)
+    save_v = pltpu.make_async_copy(V.at[:, :, core, :], vel_out, store_sem.at[0])
+    save_v.start()
+    stress_planes(e3, 0, 3, 2, 3)
+
+    some = pl.ds(0, owners - 1)
+    wait_g = whole(gathered.at[some], gathered.at[some], sum_sems.at[6], sum_sems.at[7])
     wait_g.wait_recv()
     for comp in range(2):
         for t in range(BUILDINGS // LANES):
             k = comp * (BUILDINGS // LANES) + t
             shear[comp:comp + 1, t * LANES:(t + 1) * LANES] = gathered[k // per_owner, k % per_owner]
 
+    eb3 = arrive(c, 6, V, VX, 3, NZ)
+    stress_planes(eb3, 3, NZ, 3, NZ)
+    save_s = pltpu.make_async_copy(S.at[:, :, core, :], stress_out, store_sem.at[1])
+    save_s.start()
+
     for copies in started:
         for copy in copies:
             copy.wait_send()
     all_regional.wait_send()
     wait_r1.wait_send()
-    wait_r2.wait_send()
+    for x in range(x_size):
+        @pl.when(gx != x * z_size)
+        def _():
+            down_like = whole(q1, q1, sum_sems.at[2], sum_sems.at[3])
+            down_like.wait_send()
+
+    @pl.when(is_hub)
+    def _():
+        low = whole(
+            hub.at[pl.ds(0, z_size - 1)], hub.at[pl.ds(0, z_size - 1)], sum_sems.at[4], sum_sems.at[5])
+        low.wait_send()
+
     wait_g.wait_send()
     save_v.wait()
     save_s.wait()
@@ -347,12 +453,11 @@
 
 def body(velocity, stress, zones, zone_table, regional, owner, footprint_building, footprint_block):
     GX, GY = lax.axis_size("gx"), lax.axis_size("gy")
-    nz_own = min(GX, ROWS)
-    per_owner = ROWS // nz_own
+    owners = min(GY, ROWS)
+    per_owner = ROWS // owners
     rounds = 7
     vmem = pl.BlockSpec(memory_space=pltpu.VMEM)
-    smem = pl.BlockSpec(memory_space=pltpu.SMEM)
-    hbm = pl.BlockSpec(memory_space=pl.ANY)
+    hbm = pl.BlockSpec(memory_space=pltpu.HBM)
     dma = pltpu.SemaphoreType.DMA
     return pl.pallas_call(
         kernel,
@@ -361,7 +466,7 @@
             jax.ShapeDtypeStruct(stress.shape, F32),
             jax.ShapeDtypeStruct((2, BUILDINGS), F32),
         ),
-        in_specs=[smem, smem, hbm, hbm, vmem, vmem, vmem, vmem],
+        in_specs=[hbm] * 8,
         out_specs=(hbm, hbm, vmem),
         scratch_shapes=[
             pltpu.VMEM((6, NZ, CX + 2 * PAD, CY), F32),
@@ -377,21 +482,29 @@
             pltpu.VMEM((rounds, 2, CX, CY), F32),
             pltpu.VMEM((GX, 6, 1, 2 * LANES), F32),
             pltpu.VMEM((GX, 6, 1, 2 * LANES), F32),
-            pltpu.VMEM((nz_own, per_owner, 1, LANES), F32),
+            pltpu.VMEM((owners, per_owner, 1, LANES), F32),
+            pltpu.VMEM((GY, per_owner, 1, LANES), F32),
+            pltpu.VMEM((per_owner, 1, LANES), F32),
             pltpu.VMEM((GX, per_owner, 1, LANES), F32),
             pltpu.VMEM((per_owner, 1, LANES), F32),
-            pltpu.VMEM((GY, per_owner, 1, LANES), F32),
-            pltpu.VMEM((per_owner, 1, LANES), F32),
-            pltpu.VMEM((nz_own, per_owner, 1, LANES), F32),
-            dma((2,)),
+            pltpu.VMEM((owners, per_owner, 1, LANES), F32),
+            pltpu.SMEM(owner.shape, owner.dtype),
+            pltpu.SMEM(zone_table.shape, zone_table.dtype),
+            pltpu.VMEM(zones.shape, zones.dtype),
+            pltpu.VMEM(regional.shape, regional.dtype),
+            pltpu.VMEM(footprint_building.shape, footprint_building.dtype),
+            pltpu.VMEM(footprint_block.shape, footprint_block.dtype),
+            dma((8,)),
             dma((2,)),
             dma((rounds, 4)),
             dma((rounds, 4)),
             dma((2,)),
-            dma((6,)),
+            dma((8,)),
+            pltpu.SemaphoreType.REGULAR((GX,)),
+            pltpu.SemaphoreType.REGULAR((2,)),
         ],
         compiler_params=pltpu.CompilerParams(
-            collective_id=0, has_side_effects=True, vmem_limit_bytes=32 * 1024 * 1024
+            collective_id=0, has_side_effects=True, vmem_limit_bytes=60 * 1024 * 1024
         ),
     )(owner, zone_table, velocity, stress, zones, regional, footprint_building, footprint_block)
 

time: 81.8 us -> 75.8 us (0.927)
  the two profiles are of different devices: /device:TPU:1 before, /device:TPU:6 now
where the time goes in v2:
time: 75.8 us; the launch traced here: 75.6 us
  Pallas kernels  71.6 us (94%)
  local copies, waits for them, and re-layouts  3.33 us (4%)
    pallas_call x1, Pallas kernels, body(): pl.pallas_call(kernel, out_shape=(jax.ShapeDtypeStruct(velocity.shape, F3...  71.6 us
    unnamed x7, local copies, waits for them, and re-layouts  3.33 us

profile of v2, /device:TPU:6, one launch (start us, length us, event | category | flops | bytes accessed | tf_op | source)
XLA Modules:
  0.0 75.6 jit_solution(10486320938430899150)
XLA Ops:
  0.6 71.6 %shard_map.103 = (f32[3,8,32,128]{3,2,1,0:T(8,128)}, f32[6,8,32,128]{3,2,1,0:T(8,128)}, f32[2,1024]{1,0:T(2,128)}) custom-call(s32[32]{0:T(128)} %owner_hbm.1, f32[3,16]{1,0:T(4,128)} %table_hbm.1, f32[3,8,32,128]{3,2,1,0:T(8,128)} %vel.1, f32[6,8,32,128]{3,2,1,0:T(8,128)} %stress_in.1, s32[8,32,128]{2,1,0:T(8,128)} %zones_hbm.1, ...), custom_call_target="tpu_custom_call" | custom-call | tf_op jit(solution)/shard_map/pallas_call | solution.py:462
  72.3 0.0 copy-start
  72.3 1.8 %copy.14 = f32[3,8,32,128]{3,2,1,0:T(8,128)} copy(f32[3,8,32,128]{3,2,1,0:T(8,128)} %get-tuple-element.6) | data formatting | bytes 786432
  74.1 0.0 copy-done
  74.1 0.0 copy-start.1
  74.1 0.9 %copy.15 = f32[6,8,32,128]{3,2,1,0:T(8,128)} copy(f32[6,8,32,128]{3,2,1,0:T(8,128)S(1)} %copy-done) | data formatting | bytes 1572864
  75.0 0.0 copy-done.1
  75.0 0.6 copy.16
Async XLA Ops:
  72.3 1.9 %copy-start = (f32[6,8,32,128]{3,2,1,0:T(8,128)S(1)}, f32[6,8,32,128]{3,2,1,0:T(8,128)}, u32[]{:S(2)}) copy-start(f32[6,8,32,128]{3,2,1,0:T(8,128)} %get-tuple-element.7) | copy-start | bytes 2359300
  74.1 0.9 %copy-start.1 = (f32[2,1024]{1,0:T(2,128)S(1)}, f32[2,1024]{1,0:T(2,128)}, u32[]{:S(2)}) copy-start(f32[2,1024]{1,0:T(2,128)} %get-tuple-element.8) | copy-start | bytes 24580

commit v3 on v2

v3 whole, which is shorter than its diff:
```python
import functools

import jax
import jax.numpy as jnp
from jax import lax
from jax.experimental import pallas as pl
from jax.experimental.pallas import tpu as pltpu
from jax.sharding import PartitionSpec as P

CX = 32
CY = 128
NZ = 8
STEPS = 2
COARSE = 4
BLOCK = 8
ZONES = 16
BUILDINGS = 1024
LANES = 128
PAD = 8
WIDE = 4
HIGH_ROWS = CX + 2 * PAD
GROUP = 16
ROWS = 2 * BUILDINGS // LANES
MESH = pl.DeviceIdType.MESH
HIGH = lax.Precision.HIGHEST
F32 = jnp.float32

XX, XZ, XY, YY, YZ, ZZ = range(6)


def lane_of(shape):
    return lax.broadcasted_iota(jnp.int32, shape, len(shape) - 1)


def row_of(shape):
    return lax.broadcasted_iota(jnp.int32, shape, len(shape) - 2)


def layers(gx_size):
    z_size = min(gx_size, 16)
    return z_size, gx_size // z_size


def kernel(
    owner_hbm, table_hbm, vel, stress_in, zones_hbm, regional_hbm, buildings_hbm, blocks_hbm,
    vel_out, stress_out, shear,
    S, V, lam, mu, buoy, drm, counts,
    xs, xr, ys, yr, corner, packed, block, reg_send, reg_recv, part, r1, q1, hub, q2, gathered,
    owner, table, zones, regional, buildings, blocks,
    load_sem, store_sem, halo_send, halo_recv, block_send, block_recv, reg_sems, sum_sems, entered, beside,
):
    GX, GY = lax.axis_size("gx"), lax.axis_size("gy")
    gx, gy = lax.axis_index("gx"), lax.axis_index("gy")
    z_size, x_size = layers(GX)
    owners = part.shape[0]
    z_me = gx % z_size
    base_x = gx - z_me

    def rank_of(g):
        return (g % z_size) * x_size + g // z_size

    def at_rank(q):
        return (q % x_size) * z_size + q // x_size

    me = rank_of(gx)

    core = pl.ds(PAD, CX)
    loads = [
        pltpu.make_async_copy(src, dst, load_sem.at[k]) for k, (src, dst) in enumerate([
            (stress_in, S.at[:, :, 0, core, :]), (vel, V.at[:, :, 0, core, :]), (regional_hbm, regional),
            (zones_hbm, zones), (table_hbm, table), (owner_hbm, owner), (buildings_hbm, buildings),
            (blocks_hbm, blocks),
        ])
    ]
    for load in loads:
        load.start()

    barrier = pltpu.get_barrier_semaphore()

    def greet_x(q, carry):
        pl.semaphore_signal(barrier, inc=1, device_id=(at_rank(q), gy), device_id_type=MESH)
        return carry

    def greet_y(d, carry):
        pl.semaphore_signal(barrier, inc=1, device_id=(gx, (gy + d) % GY), device_id_type=MESH)
        return carry

    after, before = (gx + 1) % GX, (gx + GX - 1) % GX
    right, left = (gy + 1) % GY, (gy + GY - 1) % GY
    sides = ((before, rank_of(before)), (after, rank_of(after)))

    for next_x, rank in sides:
        @pl.when(rank > me)
        def _():
            for y in (left, right):
                pl.semaphore_signal(barrier, inc=1, device_id=(next_x, y), device_id_type=MESH)

    lax.fori_loop(1, GY, greet_y, 0)
    lax.fori_loop(me + 1, GX, greet_x, 0)

    lane = lane_of((CX, CY))
    wide_lane = lane_of((CX + 2 * WIDE, CY))

    fields = {"s": S, "v": V, "zone": zones}
    s_planes = [("s", f, z) for f in range(6) for z in range(NZ)]
    v_planes = [("v", f, z) for f in range(3) for z in range(NZ)]
    z_planes = [("zone", 0, z) for z in range(NZ)]
    y_planes = s_planes + v_planes + z_planes

    def needed_early(plane):
        name, f, z = plane
        return z < 5 or (name == "s" and f in (XZ, YZ, ZZ) and z < 6)

    early = [p for p in y_planes if needed_early(p)]
    late = [p for p in y_planes if not needed_early(p)]
    x_planes = early + late
    n_early = len(early)

    def rows_of(plane, r, n):
        name, f, z = plane
        if name == "zone":
            return zones[z, r:r + n, :].astype(F32)
        return fields[name][f, z, 0, PAD + r:PAD + r + n, :]

    for k in (0, 1, 3):
        loads[k].wait()
    for k, plane in enumerate(x_planes):
        xs[0, k] = rows_of(plane, 0, WIDE)
        xs[1, k] = rows_of(plane, CX - WIDE, WIDE)
    for g in range(len(y_planes) // GROUP):
        acc = jnp.zeros((CX, CY), F32)
        for k in range(GROUP):
            moved = pltpu.roll(rows_of(y_planes[g * GROUP + k], 0, CX), 2 * WIDE * k + WIDE, 1)
            acc = jnp.where((lane >> 3) == k, moved, acc)
        ys[g] = acc

    e_part, l_part = pl.ds(0, n_early), pl.ds(n_early, len(late))
    top, bottom = pl.ds(0, 8), pl.ds(CX - 8, 8)
    halo = [
        pltpu.make_async_remote_copy(
            src_ref=src, dst_ref=dst, send_sem=halo_send.at[k], recv_sem=halo_recv.at[k],
            device_id=to, device_id_type=MESH)
        for k, (src, dst, to) in enumerate([
            (xs.at[0, e_part], xr.at[0, e_part], (before, gy)),
            (xs.at[1, e_part], xr.at[1, e_part], (after, gy)),
            (xs.at[0, l_part], xr.at[0, l_part], (before, gy)),
            (xs.at[1, l_part], xr.at[1, l_part], (after, gy)),
            (ys, yr.at[0], (gx, left)),
            (ys, yr.at[1], (gx, right)),
            (ys.at[:, top, :], corner.at[0, 1], (before, left)),
            (ys.at[:, top, :], corner.at[0, 0], (before, right)),
            (ys.at[:, bottom, :], corner.at[1, 1], (after, left)),
            (ys.at[:, bottom, :], corner.at[1, 0], (after, right)),
        ])
    ]
    by_side = ((0, 6, 7, 2), (1, 8, 9, 3))

    lower = [(rank < me).astype(jnp.int32) for _, rank in sides]
    pl.semaphore_wait(barrier, me + GY - 1 + 2 * (lower[0] + lower[1]))

    for side, (next_x, rank) in enumerate(sides):
        @pl.when(rank < me)
        def _():
            for k, y in enumerate((right, gy, left)):
                pl.semaphore_signal(
                    beside.at[1 - side, k], inc=1, device_id=(next_x, y), device_id_type=MESH)

    for side, (next_x, rank) in enumerate(sides):
        @pl.when(rank < me)
        def _():
            for k in by_side[side]:
                halo[k].start()

    halo[4].start()
    halo[5].start()

    def answer(q, carry):
        pl.semaphore_signal(entered.at[me], inc=1, device_id=(at_rank(q), gy), device_id_type=MESH)
        return carry

    lax.fori_loop(0, me, answer, 0)

    loads[2].wait()

    def pack_regional(i, carry):
        for s in range(STEPS):
            for c in range(3):
                reg_send[i, s * 3 + c, 0:1, :] = regional[0, s, c, pl.ds(i, 1), :]
        return carry

    lax.fori_loop(0, GX, pack_regional, 0)

    def send_regional(q):
        to = at_rank(q)
        pltpu.make_async_remote_copy(
            src_ref=reg_send.at[to], dst_ref=reg_recv.at[gx], send_sem=reg_sems.at[0],
            recv_sem=reg_sems.at[1], device_id=(to, gy), device_id_type=MESH).start()

    def send_lower(q, carry):
        send_regional(q)
        return carry

    def send_higher(q, carry):
        pl.semaphore_wait(entered.at[q], 1)
        send_regional(q)
        return carry

    lax.fori_loop(0, me, send_lower, 0)
    reg_recv[gx] = reg_send[gx]
    near = jnp.minimum(me + 1 + 3 * x_size, GX)

    for side, (next_x, rank) in enumerate(sides):
        @pl.when(rank > me)
        def _():
            for k in range(3):
                pl.semaphore_wait(beside.at[side, k], 1)
            for k in by_side[side]:
                halo[k].start()

    for k in (4, 5, 6, 7):
        loads[k].wait()

    def lookup(zone):
        bits = [(zone & (1 << b)) != 0 for b in range(4)]
        found = []
        for row in range(3):
            level = [table[row, t] * 0.1 for t in range(ZONES)]
            for b in range(4):
                level = [
                    jnp.where(bits[b], level[2 * t + 1], level[2 * t]) for t in range(len(level) // 2)
                ]
            found.append(level[0])
        return found

    materials = (lam, mu, buoy)
    for z in range(NZ):
        for target, value in zip(materials, lookup(zones[z])):
            target[z, 0, core, :] = value

    n_blocks = (CX // BLOCK) * (CY // BLOCK)
    entries = blocks.shape[-1]
    block_hot = (blocks[0] == row_of((n_blocks, entries))).astype(jnp.bfloat16)
    building_hot = (buildings[0] == row_of((BUILDINGS, entries))).astype(jnp.bfloat16)
    counts[...] = lax.dot_general(
        block_hot, building_hot, (((1,), (1,)), ((), ())), preferred_element_type=F32)

    lax.fori_loop(me + 1, near, send_higher, 0)

    def whole(src, dst, send_sem, recv_sem):
        return pltpu.make_async_remote_copy(
            src_ref=src, dst_ref=dst, send_sem=send_sem, recv_sem=recv_sem,
            device_id=((gx + 1) % GX, gy), device_id_type=MESH)

    all_regional = whole(
        reg_send.at[pl.ds(0, GX - 1)], reg_recv.at[pl.ds(0, GX - 1)], reg_sems.at[0], reg_sems.at[1])

    around = [(dx, dy) for dx in (-1, 0, 1) for dy in (-1, 0, 1) if (dx, dy) != (0, 0)]
    x_at, y_at = {-1: before, 0: gx, 1: after}, {-1: left, 0: gy, 1: right}
    share = [
        pltpu.make_async_remote_copy(
            src_ref=block.at[1, 1], dst_ref=block.at[1 - dx, 1 - dy], send_sem=block_send.at[k],
            recv_sem=block_recv.at[k], device_id=(x_at[dx], y_at[dy]), device_id_type=MESH)
        for k, (dx, dy) in enumerate(around)
    ]

    def share_block():
        all_regional.wait_recv()
        block[1, 1] = reg_recv[owner[gy]]
        for copy in share:
            copy.start()

    def spread_blocks():
        for copy in share:
            copy.wait_recv()
        wide = (HIGH_ROWS, 2 * LANES)
        row = row_of(wide)
        keep = (lane_of(wide) >> 5) == (((row - PAD) >> 2) & 7)

        def stack(y):
            parts = []
            for q in range(6):
                above, own, below = [jnp.broadcast_to(block[x, y, q], wide) for x in range(3)]
                value = jnp.where(row < PAD, above, jnp.where(row < PAD + CX, own, below))
                parts.append(jnp.where(keep, value, 0.0))
            return jnp.concatenate(parts, axis=0)

        shape = (2 * LANES, CY)
        cell, out = row_of(shape) & 31, lane_of(shape)
        own = (cell == (out >> 2)).astype(F32)
        from_left = ((cell == 31) & (out >= CY - WIDE)).astype(F32)
        from_right = ((cell == 0) & (out < WIDE)).astype(F32)
        dot = functools.partial(jnp.dot, precision=HIGH, preferred_element_type=F32)
        middle = dot(stack(1), own)
        edges = dot(stack(0), from_left) + dot(stack(2), from_right)
        for q in range(6):
            drm[q, 0] = middle[q * HIGH_ROWS:(q + 1) * HIGH_ROWS, :]
            drm[q, 1] = edges[q * HIGH_ROWS:(q + 1) * HIGH_ROWS, :]

    def take_lanes():
        second = (lane & 4) != 0
        for g in range(len(y_planes) // GROUP):
            packed[g, core, :] = jnp.where(second, yr[0, g], yr[1, g])
            packed[g, top, :] = jnp.where(second[:8], corner[1, 1, g], corner[1, 0, g])
            packed[g, pl.ds(PAD + CX, 8), :] = jnp.where(second[:8], corner[0, 1, g], corner[0, 0, g])

    def unpack(planes):
        for plane in planes:
            name, f, z = plane
            ref = fields[name]
            k = x_planes.index(plane)
            m = y_planes.index(plane)
            back = CY - (2 * WIDE * (m % GROUP) + WIDE)
            if name == "zone":
                low = lookup(xr[1, k].astype(jnp.int32))
                high = lookup(xr[0, k].astype(jnp.int32))
                for t, target in enumerate(materials):
                    target[z, 0, PAD - WIDE:PAD, :] = low[t]
                    target[z, 0, PAD + CX:PAD + CX + WIDE, :] = high[t]
                    target[z, 1] = pltpu.roll(edge_materials[t], back, 1)
            else:
                ref[f, z, 0, PAD - WIDE:PAD, :] = xr[1, k]
                ref[f, z, 0, PAD + CX:PAD + CX + WIDE, :] = xr[0, k]
                ref[f, z, 1] = pltpu.roll(packed[m // GROUP], back, 1)

    def region(last):
        return (PAD, CX) if last else (PAD - WIDE, CX + 2 * WIDE)

    def diffs(ref, f, z, c, r, n):
        def at(k, d):
            return ref[f, k, c, pl.ds(r + d, n), :]

        def dx():
            return at(z, 1) - at(z, -1)

        def dz():
            if z == 0:
                return at(1, 0)
            if z == NZ - 1:
                return -at(NZ - 2, 0)
            return at(z + 1, 0) - at(z - 1, 0)

        def dy():
            here = wide_lane[:n]
            value, other = at(z, 0), ref[f, z, 1 - c, pl.ds(r, n), :]
            up = jnp.where(here == CY - 1, pltpu.roll(other, CY - 1, 1), pltpu.roll(value, CY - 1, 1))
            down = jnp.where(here == 0, pltpu.roll(other, 1, 1), pltpu.roll(value, 1, 1))
            return up - down

        return dx, dy, dz

    def velocity_planes(step, z0, z1):
        r, n = region(False)
        here = pl.ds(r, n)
        for z in range(z0, z1):
            for c in range(2):
                b = buoy[z, c, here, :]
                dxx, dxz, dxy, dyy, dyz, dzz = [diffs(S, f, z, c, r, n) for f in range(6)]
                force = [
                    dxx[0]() + dxy[1]() + dxz[2](),
                    dxy[0]() + dyy[1]() + dyz[2](),
                    dxz[0]() + dyz[1]() + dzz[2](),
                ]
                for k in range(3):
                    f = force[k]
                    if z == NZ - 1:
                        f = f + 20.0 * mu[z, c, here, :] * drm[step * 3 + k, c, here, :]
                    V[k, z, c, here, :] = V[k, z, c, here, :] + b * f

    def stress_planes(z0, z1, last):
        r, n = region(last)
        here = pl.ds(r, n)
        for z in range(z0, z1):
            for c in range(1 if last else 2):
                vx, vy, vz = [diffs(V, f, z, c, r, n) for f in range(3)]
                m1 = mu[z, c, here, :]
                dvx, dvy, dvz = vx[0](), vy[1](), vz[2]()
                common = lam[z, c, here, :] * (dvx + dvy + dvz)
                m2 = m1 + m1
                S[XX, z, c, here, :] = S[XX, z, c, here, :] + (common + m2 * dvx)
                S[YY, z, c, here, :] = S[YY, z, c, here, :] + (common + m2 * dvy)
                S[ZZ, z, c, here, :] = S[ZZ, z, c, here, :] + (common + m2 * dvz)
                S[XZ, z, c, here, :] = S[XZ, z, c, here, :] + m1 * (vx[2]() + vz[0]())
                S[XY, z, c, here, :] = S[XY, z, c, here, :] + m1 * (vx[1]() + vy[0]())
                S[YZ, z, c, here, :] = S[YZ, z, c, here, :] + m1 * (vy[2]() + vz[1]())

    for k in (0, 1, 4, 5, 6, 7, 8, 9):
        halo[k].wait_recv()
    take_lanes()
    edge_materials = lookup(packed[len(y_planes) // GROUP - 1].astype(jnp.int32))
    unpack(early)
    velocity_planes(0, 0, 5)
    stress_planes(0, 4, False)
    velocity_planes(1, 0, 3)
    stress_planes(0, 2, True)

    sums = jnp.concatenate(
        [jnp.sum(S[f, 1, 0, core, :].reshape(CX // BLOCK, BLOCK, CY), axis=1) for f in (XZ, YZ)], axis=0)
    fold_shape = (CY, n_blocks)
    fold = ((row_of(fold_shape) >> 3) == (lane_of(fold_shape) & 15)).astype(F32)
    per_block = jnp.dot(sums, fold, precision=HIGH, preferred_element_type=F32)
    mask_shape = (8, n_blocks)
    own_row = (row_of(mask_shape) & 3) == (lane_of(mask_shape) >> 4)
    per_block = jnp.where(own_row, per_block, 0.0) * (1.0 / (BLOCK * BLOCK))
    total = jnp.dot(per_block, counts[...], precision=HIGH, preferred_element_type=F32)
    per_owner = ROWS // owners
    for comp in range(2):
        row = jnp.sum(total[4 * comp:4 * comp + 4], axis=0, keepdims=True)
        for t in range(BUILDINGS // LANES):
            k = comp * (BUILDINGS // LANES) + t
            part[k // per_owner, k % per_owner] = row[:, t * LANES:(t + 1) * LANES]

    my_row = gy % owners

    def send_part(d, carry):
        to = (gy + d) % GY
        pltpu.make_async_remote_copy(
            src_ref=part.at[to % owners], dst_ref=r1.at[gy], send_sem=sum_sems.at[0],
            recv_sem=sum_sems.at[1], device_id=(gx, to), device_id_type=MESH).start()
        return carry

    lax.fori_loop(1, GY, send_part, 0)
    r1[gy] = part[my_row]
    lax.fori_loop(near, GX, send_higher, 0)
    peers_y = pl.ds(0, GY - 1)
    wait_r1 = whole(r1.at[peers_y], r1.at[peers_y], sum_sems.at[0], sum_sems.at[1])
    wait_r1.wait_recv()
    q1[...] = jnp.sum(r1[...], axis=0)

    is_hub = z_me == 0
    for x in range(x_size):
        @pl.when(gx != x * z_size)
        def _():
            pltpu.make_async_remote_copy(
                src_ref=q1, dst_ref=hub.at[gx], send_sem=sum_sems.at[2],
                recv_sem=sum_sems.at[3], device_id=(x * z_size, gy), device_id_type=MESH).start()

    halo[2].wait_recv()
    halo[3].wait_recv()
    unpack(late)
    share_block()

    peers_x = pl.ds(0, GX - 1)
    wait_hub = whole(hub.at[peers_x], hub.at[peers_x], sum_sems.at[2], sum_sems.at[3])

    def send_down(z, carry):
        pltpu.make_async_remote_copy(
            src_ref=q2, dst_ref=q2, send_sem=sum_sems.at[4],
            recv_sem=sum_sems.at[5], device_id=(base_x + z, gy), device_id_type=MESH).start()
        return carry

    down = whole(q2, q2, sum_sems.at[4], sum_sems.at[5])

    @pl.when(is_hub)
    def _():
        hub[gx] = q1[...]
        wait_hub.wait_recv()
        q2[...] = jnp.sum(hub[...], axis=0)
        lax.fori_loop(1, z_size, send_down, 0)

    @pl.when(z_me != 0)
    def _():
        down.wait_recv()

    base = gy - my_row

    def send_total(d, carry):
        to = base + (my_row + d) % owners
        pltpu.make_async_remote_copy(
            src_ref=q2, dst_ref=gathered.at[my_row], send_sem=sum_sems.at[6],
            recv_sem=sum_sems.at[7], device_id=(gx, to), device_id_type=MESH).start()
        return carry

    lax.fori_loop(1, owners, send_total, 0)
    gathered[my_row] = q2[...]

    spread_blocks()
    velocity_planes(0, 5, NZ)
    stress_planes(4, NZ, False)
    velocity_planes(1, 3, NZ)
    save_v = pltpu.make_async_copy(V.at[:, :, 0, core, :], vel_out, store_sem.at[0])
    save_v.start()
    stress_planes(2, NZ, True)
    save_s = pltpu.make_async_copy(S.at[:, :, 0, core, :], stress_out, store_sem.at[1])
    save_s.start()

    some = pl.ds(0, owners - 1)
    wait_g = whole(gathered.at[some], gathered.at[some], sum_sems.at[6], sum_sems.at[7])
    wait_g.wait_recv()
    for comp in range(2):
        for t in range(BUILDINGS // LANES):
            k = comp * (BUILDINGS // LANES) + t
            shear[comp:comp + 1, t * LANES:(t + 1) * LANES] = gathered[k // per_owner, k % per_owner]

    for copy in halo + share:
        copy.wait_send()
    all_regional.wait_send()
    wait_r1.wait_send()
    for x in range(x_size):
        @pl.when(gx != x * z_size)
        def _():
            down_like = whole(q1, q1, sum_sems.at[2], sum_sems.at[3])
            down_like.wait_send()

    @pl.when(is_hub)
    def _():
        low = whole(
            hub.at[pl.ds(0, z_size - 1)], hub.at[pl.ds(0, z_size - 1)], sum_sems.at[4], sum_sems.at[5])
        low.wait_send()

    wait_g.wait_send()
    save_v.wait()
    save_s.wait()


def body(velocity, stress, zones, zone_table, regional, owner, footprint_building, footprint_block):
    GX, GY = lax.axis_size("gx"), lax.axis_size("gy")
    owners = min(GY, ROWS)
    per_owner = ROWS // owners
    planes = 10 * NZ
    groups = planes // GROUP
    vmem = pl.BlockSpec(memory_space=pltpu.VMEM)
    hbm = pl.BlockSpec(memory_space=pltpu.HBM)
    dma = pltpu.SemaphoreType.DMA
    return pl.pallas_call(
        kernel,
        out_shape=(
            jax.ShapeDtypeStruct(velocity.shape, F32),
            jax.ShapeDtypeStruct(stress.shape, F32),
            jax.ShapeDtypeStruct((2, BUILDINGS), F32),
        ),
        in_specs=[hbm] * 8,
        out_specs=(hbm, hbm, vmem),
        scratch_shapes=[
            pltpu.VMEM((6, NZ, 2, HIGH_ROWS, CY), F32),
            pltpu.VMEM((3, NZ, 2, HIGH_ROWS, CY), F32),
            pltpu.VMEM((NZ, 2, HIGH_ROWS, CY), F32),
            pltpu.VMEM((NZ, 2, HIGH_ROWS, CY), F32),
            pltpu.VMEM((NZ, 2, HIGH_ROWS, CY), F32),
            pltpu.VMEM((6, 2, HIGH_ROWS, CY), F32),
            pltpu.VMEM((64, BUILDINGS), F32),
            pltpu.VMEM((2, planes, WIDE, CY), F32),
            pltpu.VMEM((2, planes, WIDE, CY), F32),
            pltpu.VMEM((groups, CX, CY), F32),
            pltpu.VMEM((2, groups, CX, CY), F32),
            pltpu.VMEM((2, 2, groups, 8, CY), F32),
            pltpu.VMEM((groups, HIGH_ROWS, CY), F32),
            pltpu.VMEM((3, 3, 6, 1, 2 * LANES), F32),
            pltpu.VMEM((GX, 6, 1, 2 * LANES), F32),
            pltpu.VMEM((GX, 6, 1, 2 * LANES), F32),
            pltpu.VMEM((owners, per_owner, 1, LANES), F32),
            pltpu.VMEM((GY, per_owner, 1, LANES), F32),
            pltpu.VMEM((per_owner, 1, LANES), F32),
            pltpu.VMEM((GX, per_owner, 1, LANES), F32),
            pltpu.VMEM((per_owner, 1, LANES), F32),
            pltpu.VMEM((owners, per_owner, 1, LANES), F32),
            pltpu.SMEM(owner.shape, owner.dtype),
            pltpu.SMEM(zone_table.shape, zone_table.dtype),
            pltpu.VMEM(zones.shape, zones.dtype),
            pltpu.VMEM(regional.shape, regional.dtype),
            pltpu.VMEM(footprint_building.shape, footprint_building.dtype),
            pltpu.VMEM(footprint_block.shape, footprint_block.dtype),
            dma((8,)),
            dma((2,)),
            dma((10,)),
            dma((10,)),
            dma((8,)),
            dma((8,)),
            dma((2,)),
            dma((8,)),
            pltpu.SemaphoreType.REGULAR((GX,)),
            pltpu.SemaphoreType.REGULAR((2, 3)),
        ],
        compiler_params=pltpu.CompilerParams(
            collective_id=0, has_side_effects=True, vmem_limit_bytes=60 * 1024 * 1024
        ),
    )(owner, zone_table, velocity, stress, zones, regional, footprint_building, footprint_block)


def solution(mesh):
    return jax.shard_map(
        body,
        mesh=mesh,
        in_specs=(
            P(None, None, "gx", "gy"),
            P(None, None, "gx", "gy"),
            P(None, "gx", "gy"),
            P(),
            P("gx", None, None, None, "gy"),
            P(),
            P("gx", "gy", None),
            P("gx", "gy", None),
        ),
        out_specs=(P(None, None, "gx", "gy"), P(None, None, "gx", "gy"), P()),
        check_vma=False,
    )
```

time: 75.8 us -> 63 us (0.83)
  the two profiles are of different devices: /device:TPU:6 before, /device:TPU:1 now
where the time goes in v3:
time: 63 us; the launch traced here: 62.8 us
  Pallas kernels  58.8 us (93%)
  local copies, waits for them, and re-layouts  3.33 us (5%)
  between operations  0.65 us (1%)
    pallas_call x1, Pallas kernels, body(): pl.pallas_call(kernel, out_shape=(jax.ShapeDtypeStruct(velocity.shape, F3...  58.8 us
    unnamed x7, local copies, waits for them, and re-layouts  3.33 us

profile of v3, /device:TPU:1, one launch (start us, length us, event | category | flops | bytes accessed | tf_op | source)
XLA Modules:
  0.0 62.8 jit_solution(7603697774879523745)
XLA Ops:
  0.6 58.8 %shard_map.103 = (f32[3,8,32,128]{3,2,1,0:T(8,128)}, f32[6,8,32,128]{3,2,1,0:T(8,128)}, f32[2,1024]{1,0:T(2,128)}) custom-call(s32[32]{0:T(128)} %owner_hbm.1, f32[3,16]{1,0:T(4,128)} %table_hbm.1, f32[3,8,32,128]{3,2,1,0:T(8,128)} %vel.1, f32[6,8,32,128]{3,2,1,0:T(8,128)} %stress_in.1, s32[8,32,128]{2,1,0:T(8,128)} %zones_hbm.1, ...), custom_call_target="tpu_custom_call" | custom-call | tf_op jit(solution)/shard_map/pallas_call | solution.py:524
  59.5 0.0 copy-start
  59.5 1.8 %copy.14 = f32[3,8,32,128]{3,2,1,0:T(8,128)} copy(f32[3,8,32,128]{3,2,1,0:T(8,128)} %get-tuple-element.6) | data formatting | bytes 786432
  61.3 0.0 copy-done
  61.3 0.0 copy-start.1
  61.3 0.9 %copy.15 = f32[6,8,32,128]{3,2,1,0:T(8,128)} copy(f32[6,8,32,128]{3,2,1,0:T(8,128)S(1)} %copy-done) | data formatting | bytes 1572864
  62.2 0.0 copy-done.1
  62.2 0.6 copy.16
Async XLA Ops:
  59.5 1.9 %copy-start = (f32[6,8,32,128]{3,2,1,0:T(8,128)S(1)}, f32[6,8,32,128]{3,2,1,0:T(8,128)}, u32[]{:S(2)}) copy-start(f32[6,8,32,128]{3,2,1,0:T(8,128)} %get-tuple-element.7) | copy-start | bytes 2359300
  61.3 0.9 %copy-start.1 = (f32[2,1024]{1,0:T(2,128)S(1)}, f32[2,1024]{1,0:T(2,128)}, u32[]{:S(2)}) copy-start(f32[2,1024]{1,0:T(2,128)} %get-tuple-element.8) | copy-start | bytes 24580

commit v4 on v3

--- a/solution.py
+++ b/solution.py
@@ -97,6 +97,22 @@
 
     lax.fori_loop(1, GY, greet_y, 0)
     lax.fori_loop(me + 1, GX, greet_x, 0)
+
+    lower = [(rank < me).astype(jnp.int32) for _, rank in sides]
+    pl.semaphore_wait(barrier, me + GY - 1 + 2 * (lower[0] + lower[1]))
+
+    for side, (next_x, rank) in enumerate(sides):
+        @pl.when(rank < me)
+        def _():
+            for k, y in enumerate((right, gy, left)):
+                pl.semaphore_signal(
+                    beside.at[1 - side, k], inc=1, device_id=(next_x, y), device_id_type=MESH)
+
+    def answer(q, carry):
+        pl.semaphore_signal(entered.at[me], inc=1, device_id=(at_rank(q), gy), device_id_type=MESH)
+        return carry
+
+    lax.fori_loop(0, me, answer, 0)
 
     lane = lane_of((CX, CY))
     wide_lane = lane_of((CX + 2 * WIDE, CY))
@@ -155,16 +171,6 @@
     ]
     by_side = ((0, 6, 7, 2), (1, 8, 9, 3))
 
-    lower = [(rank < me).astype(jnp.int32) for _, rank in sides]
-    pl.semaphore_wait(barrier, me + GY - 1 + 2 * (lower[0] + lower[1]))
-
-    for side, (next_x, rank) in enumerate(sides):
-        @pl.when(rank < me)
-        def _():
-            for k, y in enumerate((right, gy, left)):
-                pl.semaphore_signal(
-                    beside.at[1 - side, k], inc=1, device_id=(next_x, y), device_id_type=MESH)
-
     for side, (next_x, rank) in enumerate(sides):
         @pl.when(rank < me)
         def _():
@@ -174,12 +180,6 @@
     halo[4].start()
     halo[5].start()
 
-    def answer(q, carry):
-        pl.semaphore_signal(entered.at[me], inc=1, device_id=(at_rank(q), gy), device_id_type=MESH)
-        return carry
-
-    lax.fori_loop(0, me, answer, 0)
-
     loads[2].wait()
 
     def pack_regional(i, carry):
@@ -196,6 +196,9 @@
             src_ref=reg_send.at[to], dst_ref=reg_recv.at[gx], send_sem=reg_sems.at[0],
             recv_sem=reg_sems.at[1], device_id=(to, gy), device_id_type=MESH).start()
 
+    first_layer = 1 - jnp.minimum(z_me, 1)
+    near = jnp.minimum(me + 1 + 3 * x_size + first_layer * GX, GX)
+
     def send_lower(q, carry):
         send_regional(q)
         return carry
@@ -207,7 +210,6 @@
 
     lax.fori_loop(0, me, send_lower, 0)
     reg_recv[gx] = reg_send[gx]
-    near = jnp.minimum(me + 1 + 3 * x_size, GX)
 
     for side, (next_x, rank) in enumerate(sides):
         @pl.when(rank > me)
@@ -342,8 +344,8 @@
         def dy():
             here = wide_lane[:n]
             value, other = at(z, 0), ref[f, z, 1 - c, pl.ds(r, n), :]
-            up = jnp.where(here == CY - 1, pltpu.roll(other, CY - 1, 1), pltpu.roll(value, CY - 1, 1))
-            down = jnp.where(here == 0, pltpu.roll(other, 1, 1), pltpu.roll(value, 1, 1))
+            up = pltpu.roll(jnp.where(here == 0, other, value), CY - 1, 1)
+            down = pltpu.roll(jnp.where(here == CY - 1, other, value), 1, 1)
             return up - down
 
         return dx, dy, dz
@@ -434,9 +436,6 @@
                 src_ref=q1, dst_ref=hub.at[gx], send_sem=sum_sems.at[2],
                 recv_sem=sum_sems.at[3], device_id=(x * z_size, gy), device_id_type=MESH).start()
 
-    halo[2].wait_recv()
-    halo[3].wait_recv()
-    unpack(late)
     share_block()
 
     peers_x = pl.ds(0, GX - 1)
@@ -473,6 +472,9 @@
     lax.fori_loop(1, owners, send_total, 0)
     gathered[my_row] = q2[...]
 
+    halo[2].wait_recv()
+    halo[3].wait_recv()
+    unpack(late)
     spread_blocks()
     velocity_planes(0, 5, NZ)
     stress_planes(4, NZ, False)
@@ -512,6 +514,26 @@
     save_s.wait()
 
 
+def move(v_in, s_in, b_in, v_out, s_out, b_out, v_mid, s_mid, b_mid, read_sem, write_sem):
+    steps = []
+    for src, mid, dst in ((b_in, b_mid, b_out), (v_in, v_mid, v_out), (s_in, s_mid, s_out)):
+        parts = src.shape[0] if len(src.shape) > 2 else 1
+        for k in range(parts):
+            part = (src.at[k], mid.at[k], dst.at[k]) if parts > 1 else (src, mid, dst)
+            n = len(steps)
+            steps.append((
+                pltpu.make_async_copy(part[0], part[1], read_sem.at[n]),
+                pltpu.make_async_copy(part[1], part[2], write_sem.at[n]),
+            ))
+    for read, _ in steps:
+        read.start()
+    for read, write in steps:
+        read.wait()
+        write.start()
+    for _, write in steps:
+        write.wait()
+
+
 def body(velocity, stress, zones, zone_table, regional, owner, footprint_building, footprint_block):
     GX, GY = lax.axis_size("gx"), lax.axis_size("gy")
     owners = min(GY, ROWS)
@@ -521,7 +543,7 @@
     vmem = pl.BlockSpec(memory_space=pltpu.VMEM)
     hbm = pl.BlockSpec(memory_space=pltpu.HBM)
     dma = pltpu.SemaphoreType.DMA
-    return pl.pallas_call(
+    results = pl.pallas_call(
         kernel,
         out_shape=(
             jax.ShapeDtypeStruct(velocity.shape, F32),
@@ -574,6 +596,14 @@
             collective_id=0, has_side_effects=True, vmem_limit_bytes=60 * 1024 * 1024
         ),
     )(owner, zone_table, velocity, stress, zones, regional, footprint_building, footprint_block)
+    return pl.pallas_call(
+        move,
+        out_shape=tuple(jax.ShapeDtypeStruct(r.shape, r.dtype) for r in results),
+        in_specs=[hbm] * 3,
+        out_specs=(hbm,) * 3,
+        scratch_shapes=[pltpu.VMEM(r.shape, r.dtype) for r in results] + [dma((10,)), dma((10,))],
+        compiler_params=pltpu.CompilerParams(vmem_limit_bytes=60 * 1024 * 1024),
+    )(*results)
 
 
 def solution(mesh):

time: 63 us -> 62 us (0.984)
  local copies, waits for them, and re-layouts: 3.33 us -> 0 us
  Pallas kernels: 58.8 us -> 61.1 us
    unnamed x7 -> x0, local copies, waits for them, and re-layouts: 3.33 us -> none
    pallas_call x0 -> x1, Pallas kernels: none -> 2.18 us  [body(): pl.pallas_call(move, out_shape=tuple((jax.ShapeDtypeStruct(r.shape, r.dty...]
where the time goes in v4:
time: 62 us; the launch traced here: 61.7 us
  Pallas kernels  61.1 us (99%)
  between operations  0.64 us (1%)
    pallas_call x1, Pallas kernels, body(): pl.pallas_call(kernel, out_shape=(jax.ShapeDtypeStruct(velocity.shape, F3...  58.9 us
    pallas_call x1, Pallas kernels, body(): pl.pallas_call(move, out_shape=tuple((jax.ShapeDtypeStruct(r.shape, r.dty...  2.18 us

profile of v4, /device:TPU:1, one launch (start us, length us, event | category | flops | bytes accessed | tf_op | source)
XLA Modules:
  0.0 61.7 jit_solution(12468189784788476948)
XLA Ops:
  0.6 58.9 %shard_map.103 = (f32[3,8,32,128]{3,2,1,0:T(8,128)}, f32[6,8,32,128]{3,2,1,0:T(8,128)}, f32[2,1024]{1,0:T(2,128)}) custom-call(s32[32]{0:T(128)} %owner_hbm.1, f32[3,16]{1,0:T(4,128)} %table_hbm.1, f32[3,8,32,128]{3,2,1,0:T(8,128)} %vel.1, f32[6,8,32,128]{3,2,1,0:T(8,128)} %stress_in.1, s32[8,32,128]{2,1,0:T(8,128)} %zones_hbm.1, ...), custom_call_target="tpu_custom_call" | custom-call | tf_op jit(solution)/shard_map/pallas_call | solution.py:546
  59.6 2.2 %shard_map.104 = (f32[3,8,32,128]{3,2,1,0:T(8,128)}, f32[6,8,32,128]{3,2,1,0:T(8,128)}, f32[2,1024]{1,0:T(2,128)}) custom-call(f32[3,8,32,128]{3,2,1,0:T(8,128)} %get-tuple-element.6.v_in, f32[6,8,32,128]{3,2,1,0:T(8,128)} %get-tuple-element.7.s_in, f32[2,1024]{1,0:T(2,128)} %get-tuple-element.8.b_in), custom_call_target="tpu_custom_call" | custom-call | tf_op jit(solution)/shard_map/pallas_call | solution.py:599
